TPU v7x, 256 devices: a whole 4x4x8 slice. The times are simulated.
256 devices in a mesh: row: 8 (over y, core), col: 32 (over z, x).
Axes of the slice: x: 4, y: 4, z: 8, core: 2. Of those that a mesh axis runs over, the one named last changes fastest.
Arguments:
- modes: float32 [48, 2, 64, 4096], P(None, None, 'row', 'col'), may hold values from -25 to 25
- mean_flow: float32 [2, 64, 4096], P(None, 'row', 'col'), may hold values from -5 to 5
- seeds: int32 [32768, 48], P(('row', 'col')), may hold values from 0 to 4095
- amplitudes: float32 [48], replicated, may hold values from 0.5 to 2
- water_mask: int32 [64, 4096], P('row', 'col'), may hold values 0 or 1
Outputs:
- new_modes: float32 [48, 2, 64, 4096], P(None, None, 'row', 'col')
- new_coeffs: float32 [32768, 48], P(('row', 'col'))
Inputs may be any that keep to these rules, and one draw needn't show every extreme that they name: `water_mask`: 1 marks a water cell, 0 a land cell.
All inputs are finite; a program needn't handle non-finite values. No bound on the sum of `water_mask` on one device may be relied on, other than what follows from the above.
Results may differ from a plain program's by a relative error of at most 0.0003.
Values sent between devices are 32-bit elements; how exact they have to be, the bound alone decides.
A program may use at most 128 MiB of HBM per device.

v0:
```python
import math

import jax
import jax.numpy as jnp
from jax import lax
from jax.sharding import PartitionSpec as P

TIME_STEP = 0.25
VISCOUS = 0.2
PRECISE = lax.Precision.HIGHEST
BLOCK_MODES = 8


def with_halo(cells, sides, width):
    for axis, dim in sides:
        count = lax.axis_size(axis)
        ends = count - 1
        head = lax.slice_in_dim(cells, 0, width, axis=dim)
        tail = lax.slice_in_dim(cells, cells.shape[dim] - width, cells.shape[dim], axis=dim)
        cells = jnp.concatenate(
            [
                lax.ppermute(tail, axis, [(i, (i + 1) % count) for i in range(ends)]),
                cells,
                lax.ppermute(head, axis, [((i + 1) % count, i) for i in range(ends)]),
            ],
            axis=dim,
        )
    return cells


def matmul(left_side, right_side):
    return jnp.dot(left_side, right_side, precision=PRECISE, preferred_element_type=jnp.float32)


def matmul_nt(left_side, right_side):
    return lax.dot_general(
        left_side,
        right_side,
        (((1,), (1,)), ((), ())),
        precision=PRECISE,
        preferred_element_type=jnp.float32,
    )


def factor_solve(factor, right_side):
    lower_part = lax.linalg.triangular_solve(factor, right_side, left_side=True, lower=True)
    return lax.linalg.triangular_solve(
        factor, lower_part, left_side=True, lower=True, transpose_a=True
    )


def raw_coeffs(seeds, amplitudes, first_row, row_total):
    phases = seeds.astype(jnp.float32) * (3.0 * math.pi / 8192.0)
    row_ids = (first_row + jnp.arange(seeds.shape[0], dtype=jnp.int32)).astype(jnp.float32)
    strength = 0.5 + row_ids / row_total
    return strength[:, None] * amplitudes[None, :] * (jnp.cos(phases) + 0.5 * jnp.cos(2.0 * phases))


def pair_products(coeffs):
    return (coeffs[:, :, None] * coeffs[:, None, :]).reshape(coeffs.shape[0], -1)


def derivatives(padded):
    along_x = 0.5 * (padded[:, :, 2:, 1:-1] - padded[:, :, :-2, 1:-1])
    along_y = 0.5 * (padded[:, :, 1:-1, 2:] - padded[:, :, 1:-1, :-2])
    return (along_x, along_y)


def transport_term(advecting_velocity, gradient_east, gradient_north):
    return (
        advecting_velocity[..., 0:1, :, :] * gradient_east
        + advecting_velocity[..., 1:2, :, :] * gradient_north
    )


def on_device(modes, mean_flow, seeds, amplitudes, water_mask):
    mode_count = modes.shape[0]
    rows_dev = seeds.shape[0]
    row_total = rows_dev * lax.axis_size("row") * lax.axis_size("col")
    grid_total = modes.shape[2] * lax.axis_size("row") * modes.shape[3] * lax.axis_size("col")
    weight_scale = 1.0 / (2.0 * grid_total)
    first_row = lax.axis_index(("row", "col")) * rows_dev
    uncentered = raw_coeffs(seeds, amplitudes, first_row, row_total)
    column_sum = lax.psum(jnp.sum(uncentered, axis=0), ("row", "col"))
    coeffs = uncentered - column_sum / row_total
    pair_terms = pair_products(coeffs)
    local_second = matmul(coeffs.T, coeffs)
    local_third = matmul(coeffs.T, pair_terms)
    second, third_sum = lax.psum((local_second, local_third), ("row", "col"))
    covariance = second / row_total
    third_moment = third_sum / row_total
    weight_map = factor_solve(jnp.linalg.cholesky(covariance), third_moment)
    weight_cube = weight_map.reshape(mode_count, mode_count, mode_count)
    stacked_fields = jnp.concatenate([modes, mean_flow[None]], axis=0)
    padded = with_halo(stacked_fields, (("row", 2), ("col", 3)), 1)
    water_cells = water_mask.astype(jnp.float32)
    cell_weights = water_cells * weight_scale
    grad_x, grad_y = derivatives(padded)
    mode_grad_x = grad_x[:mode_count]
    mode_grad_y = grad_y[:mode_count]
    linear = -(
        transport_term(mean_flow, mode_grad_x, mode_grad_y)
        + transport_term(modes, grad_x[mode_count:], grad_y[mode_count:])
    )
    flat_values = modes.reshape(mode_count, -1)
    weighted = (modes * cell_weights).reshape(mode_count, -1)
    gram_part = matmul_nt(weighted, flat_values)
    lin_part = matmul_nt(weighted, linear.reshape(mode_count, -1))
    nonlinear = jnp.zeros_like(flat_values)
    tensor_parts = []
    for offset in range(0, mode_count, BLOCK_MODES):
        mode_block = modes[offset : offset + BLOCK_MODES]
        pair_field = (
            mode_block[:, None, 0:1] * mode_grad_x[None]
            + mode_block[:, None, 1:2] * mode_grad_y[None]
        ).reshape(BLOCK_MODES * mode_count, -1)
        tensor_parts.append(-matmul_nt(weighted, pair_field))
        weight_block = weight_cube[:, offset : offset + BLOCK_MODES, :].reshape(mode_count, -1)
        nonlinear = nonlinear + matmul(weight_block, pair_field)
    tensor_contribution = jnp.concatenate(tensor_parts, axis=1)
    gram_matrix, linear_projection, tensor = lax.psum(
        (gram_part, lin_part, tensor_contribution), ("row", "col")
    )
    forcing = water_cells * (linear - nonlinear.reshape(modes.shape))
    projected = lax.psum(matmul_nt(weighted, forcing.reshape(mode_count, -1)), ("row", "col"))
    factor = jnp.linalg.cholesky(gram_matrix)
    solved = factor_solve(factor, projected)
    correction = matmul(solved.T, flat_values).reshape(modes.shape)
    half_step = water_cells * (modes + TIME_STEP * (forcing - correction))
    beside_all = with_halo(half_step, (("row", 2), ("col", 3)), 1)
    laplace_term = (
        beside_all[:, :, 2:, 1:-1]
        + beside_all[:, :, :-2, 1:-1]
        + beside_all[:, :, 1:-1, 2:]
        + beside_all[:, :, 1:-1, :-2]
        - 4.0 * half_step
    )
    new_modes = water_cells * (half_step + VISCOUS * laplace_term)
    drift = matmul(coeffs, linear_projection.T) + matmul(
        pair_terms - covariance.reshape(1, -1), tensor.T
    )
    change = factor_solve(factor, drift.T).T
    new_coeffs = coeffs + TIME_STEP * change
    return (new_modes, new_coeffs)


def solution(mesh):
    return jax.shard_map(
        on_device,
        mesh=mesh,
        in_specs=(
            P(None, None, "row", "col"),
            P(None, "row", "col"),
            P(("row", "col"), None),
            P(),
            P("row", "col"),
        ),
        out_specs=(P(None, None, "row", "col"), P(("row", "col"), None)),
        check_vma=False,
    )
```

profile of v0, /device:TPU:1, one launch (start us, length us, event | category | flops | bytes accessed | tf_op | source)
XLA Modules:
  0.0 676.6 jit_solution(17730745178588972139)
XLA Ops:
  9.2 5.1 collective-permute-start
  20.7 78.6 %psum.49 = f32[48]{0:T(128)S(1)} all-reduce(f32[48]{0:T(128)S(1)} %fusion.61), channel_id=1, replica_groups=mesh['row'=8,'col'=32] {'row','col'}, use_global_device_ids=true, to_apply=%region_1.0 | all-reduce | flops 48 | bytes 384 | tf_op jit(solution)/shard_map/psum | solution.py:84
  103.5 73.4 %psum.50 = f32[48,48]{0,1:T(8,128)S(1)} all-reduce(f32[48,48]{0,1:T(8,128)S(1)} %fusion.68), channel_id=1, replica_groups=mesh['row'=8,'col'=32] {'row','col'}, use_global_device_ids=true, to_apply=%region_2.0 | all-reduce | flops 2304 | bytes 18432 | tf_op jit(solution)/shard_map/psum | solution.py:89
  177.0 4.4 cholesky.44
  183.6 4.0 collective-permute-start.3
  190.9 7.0 %multiply_add_fusion = (f32[8,48,2,8,128]{4,3,2,1,0:T(8,128)}, f32[8,48,2,8,128]{4,3,2,1,0:T(8,128)}, f32[8,48,2,8,128]{4,3,2,1,0:T(8,128)}, f32[8,48,2,8,128]{4...) fusion(f32[8,8,128]{2,1,0:T(8,128)S(1)} %copy-done.20, f32[8,8,128]{2,1,0:T(8,128)S(1)} %copy-done.19, ...), kind=kLoop, calls=%fused_computation | loop fusion | flops 14155776 | bytes 20054016 | tf_op jit(solution)/shard_map/add | solution.py:114
  197.8 4.6 add.216
  202.4 4.6 add.218
  207.0 4.6 add.221
  211.5 4.6 add.224
  221.4 5.7 fusion.11
  234.5 3.7 fusion.8
  238.2 3.7 fusion.7
  241.9 4.0 fusion.6
  247.9 5.0 custom-call.16
  259.2 245.2 %all-reduce.4.cloned.1.call-done = (f32[48,2304]{1,0:T(8,128)}, f32[48,2304]{1,0:T(8,128)}) async-done(((f32[48,2304]{1,0:T(8,128)}, f32[48,2304]{1,0:T(8,128)}), (f32[48,2304]{1,0:T(8,128)}, f32[48,2304]{1,0:T(8,128)})) %all-reduce.4.cloned.1.call-update) | async-done | bytes 884752 | tf_op jit(solution)/shard_map/psum | solution.py:89
  511.0 4.8 fusion.57
  519.3 4.7 fusion.70
  539.8 4.1 convolution_add_fusion.4
  543.9 4.2 convolution_add_fusion.3
  555.0 77.5 %all-reduce = (f32[48,48]{1,0:T(8,128)S(1)}, f32[48,48]{0,1:T(8,128)S(1)}, f32[48,48]{1,0:T(8,128)S(1)}) all-reduce(f32[48,48]{1,0:T(8,128)S(1)} %convolution_bitcast_fusion.2, f32[48,48]{0,1:T(8,128)} %convolution_bitcast_fusion.3, f32[48,48]{1,0:T(8,128)} %convolution_bitcast_fusion), channel_id=1, replica_groups=mesh['row'=8,'col'=32] {'row','col'}, use_global_device_ids=true, to_apply=%region_7.0 | all-reduce | flops 6912 | bytes 55296 | tf_op jit(solution)/shard_map/psum | solution.py:125
  633.5 4.4 cholesky.55
  653.8 4.0 collective-permute-start.7
  658.6 8.8 %collective-permute-done.6 = f32[48,2,10,1]{3,0,2,1:T(8,128)S(1)} collective-permute-done((f32[48,2,10,1]{3,0,2,1:T(8,128)S(1)}, f32[48,2,10,1]{3,0,2,1:T(8,128)S(1)}, u32[]{:S(2)}, u32[]{:S(2)}) %collective-permute-start.6) | collective-permute-done | bytes 3872 | tf_op jit(solution)/shard_map/ppermute | solution.py:24
  (163 shorter events, 90.8 us)
Async XLA Ops:
  7.2 93.4 %copy-start.6 = (f32[48,2,8,128]{3,2,1,0:T(8,128)S(1)}, f32[48,2,8,128]{3,2,1,0:T(8,128)}, u32[]{:S(2)}) copy-start(f32[48,2,8,128]{3,2,1,0:T(8,128)} %param.6) | copy-start | bytes 1179652
  7.2 93.4 %copy-start.32 = (s32[8,128]{1,0:T(8,128)S(1)}, s32[8,128]{1,0:T(8,128)}, u32[]{:S(2)}) copy-start(s32[8,128]{1,0:T(8,128)} %param.10) | copy-start | bytes 12292
  7.2 497.3 %all-reduce.4.cloned.1.call-start = ((), (), s32[]{:S(2)}) async-start(), calls=%async_computation | async-start | bytes 1769472 | tf_op jit(solution)/shard_map/psum | solution.py:89
  8.4 173.0 %copy-start.18 = (f32[2,8,128]{2,1,0:T(8,128)S(1)}, f32[2,8,128]{2,1,0:T(8,128)}, u32[]{:S(2)}) copy-start(f32[2,8,128]{2,1,0:T(8,128)} %param.7) | copy-start | bytes 24580
  9.2 172.2 %collective-permute-start = (f32[49,2,1,128]{3,0,2,1:T(8,128)S(1)}, f32[49,2,1,128]{3,0,2,1:T(8,128)S(1)}, u32[]{:S(2)}, u32[]{:S(2)}) collective-permute-start(f32[49,2,1,128]{3,0,2,1:T(8,128)S(1)} %get-tuple-element.36), channel_id=1, source_target_pairs={{32,0},{64,32},{96,64},{128,96},{160,128},{192,160},{224,192},{33,... | collective-permute-start | bytes 150536 | tf_op jit(solution)/shard_map/ppermute | solution.py:24
  14.3 167.1 %collective-permute-start.1 = (f32[49,2,1,128]{3,0,2,1:T(8,128)S(1)}, f32[49,2,1,128]{3,0,2,1:T(8,128)S(1)}, u32[]{:S(2)}, u32[]{:S(2)}) collective-permute-start(f32[49,2,1,128]{3,0,2,1:T(8,128)S(1)} %get-tuple-element.35), channel_id=1, source_target_pairs={{0,32},{32,64},{64,96},{96,128},{128,160},{160,192},{192,224},{1,3... | collective-permute-start | bytes 150536 | tf_op jit(solution)/shard_map/ppermute | solution.py:22
  181.4 6.9 %copy-start.31 = (f32[48,48]{1,0:T(8,128)}, f32[48,48]{1,0:T(8,128)S(1)}, u32[]{:S(2)}) copy-start(f32[48,48]{1,0:T(8,128)S(1)} %cholesky.44) | copy-start | bytes 27652
  182.0 6.3 collective-permute-start.2
  183.6 5.1 collective-permute-start.3
  221.4 5.7 copy-start.5
  221.4 9.4 %copy-start.4 = (f32[384,2048]{1,0:T(8,128)S(1)}, f32[384,2048]{1,0:T(8,128)}, u32[]{:S(2)}) copy-start(f32[384,2048]{1,0:T(8,128)} %add.221) | copy-start | bytes 9437188
  227.1 7.4 %copy-start.2 = (f32[384,2048]{1,0:T(8,128)S(1)}, f32[384,2048]{1,0:T(8,128)}, u32[]{:S(2)}) copy-start(f32[384,2048]{1,0:T(8,128)} %add.224) | copy-start | bytes 9437188
  230.8 7.4 %copy-start = (f32[384,2048]{1,0:T(8,128)S(1)}, f32[384,2048]{1,0:T(8,128)}, u32[]{:S(2)}) copy-start(f32[384,2048]{1,0:T(8,128)} %add.227) | copy-start | bytes 9437188
  539.8 8.3 %copy-start.3 = (f32[384,2048]{1,0:T(8,128)S(1)}, f32[384,2048]{1,0:T(8,128)}, u32[]{:S(2)}) copy-start(f32[384,2048]{1,0:T(8,128)} %add.224) | copy-start | bytes 9437188
  539.8 8.4 %copy-start.15 = (f32[48,384]{1,0:T(8,128)S(1)}, f32[48,384]{1,0:T(8,128)}, u32[]{:S(2)}) copy-start(f32[48,384]{1,0:T(8,128)} %reshape.245) | copy-start | bytes 221188
  543.9 6.3 copy-start.1
  543.9 6.3 copy-start.16
  554.2 96.8 %copy-start.8 = (f32[128,48,48]{0,2,1:T(8,128)S(1)}, f32[128,48,48]{0,2,1:T(8,128)}, u32[]{:S(2)}) copy-start(f32[128,48,48]{0,2,1:T(8,128)} %copy-done.7) | copy-start | bytes 3538948
  554.2 96.8 %copy-start.13 = (f32[48,2304]{1,0:T(8,128)S(1)}, f32[48,2304]{1,0:T(8,128)}, u32[]{:S(2)}) copy-start(f32[48,2304]{1,0:T(8,128)} %get-tuple-element.13) | copy-start | bytes 1327108
  643.4 14.4 %copy-start.11 = (f32[128,48]{0,1:T(8,128)S(1)}, f32[128,48]{0,1:T(8,128)}, u32[]{:S(2)}) copy-start(f32[128,48]{0,1:T(8,128)} %copy-done.10) | copy-start | bytes 73732
  645.4 6.8 collective-permute-start.4
  648.3 3.9 collective-permute-start.5
  652.5 14.9 %collective-permute-start.6 = (f32[48,2,10,1]{3,0,2,1:T(8,128)S(1)}, f32[48,2,10,1]{3,0,2,1:T(8,128)S(1)}, u32[]{:S(2)}, u32[]{:S(2)}) collective-permute-start(f32[48,2,10,1]{3,0,2,1:T(8,128)S(1)} %get-tuple-element.30), channel_id=1, source_target_pairs={{1,0},{2,1},{3,2},{4,3},{5,4},{6,5},{7,6},{8,7},{9,8},{10,9},{11,1... | collective-permute-start | bytes 11528 | tf_op jit(solution)/shard_map/ppermute | solution.py:24
  653.8 14.5 %collective-permute-start.7 = (f32[48,2,10,1]{3,0,2,1:T(8,128)S(1)}, f32[48,2,10,1]{3,0,2,1:T(8,128)S(1)}, u32[]{:S(2)}, u32[]{:S(2)}) collective-permute-start(f32[48,2,10,1]{3,0,2,1:T(8,128)S(1)} %get-tuple-element.31), channel_id=1, source_target_pairs={{0,1},{1,2},{2,3},{3,4},{4,5},{5,6},{6,7},{7,8},{8,9},{9,10},{10,1... | collective-permute-start | bytes 11528 | tf_op jit(solution)/shard_map/ppermute | solution.py:22
  (18 other events, 37.9 us)
Sparse Core Ops, SparseCore 0:
  246.1 258.3 all-reduce.3
where the time goes:
time: 688 us; the launch traced here: 677 us
  waiting for transfers between devices  255 us (37%)
  blocking collectives  230 us (33%)
  matrix products  63.3 us (9%)
  local copies, waits for them, and re-layouts  55.7 us (8%)
  other arithmetic  34.8 us (5%)
  starting transfers between devices  23.2 us (3%)
  between operations  15 us (2%)
    psum x1, waiting for transfers between devices, on_device(): second, third_sum = lax.psum((local_second, local_third), ('row', 'col'))  245 us
    psum x1, blocking collectives, on_device(): column_sum = lax.psum(jnp.sum(uncentered, axis=0), ('row', 'col'))  78.6 us
    psum x1, blocking collectives, on_device(): lax.psum(matmul_nt(weighted, forcing.reshape(mode_count, -1)), ('row', 'c...  77.5 us
    psum x1, blocking collectives, on_device(): second, third_sum = lax.psum((local_second, local_third), ('row', 'col'))  73.4 us
    dot_general x9, matrix products, matmul_nt(): lax.dot_general(left_side, right_side, (((1,), (1,)), ((), ())), precisio...  29.6 us
    dot_general x11, matrix products, matmul(): jnp.dot(left_side, right_side, precision=PRECISE, preferred_element_type=...  25.1 us
    add x6, local copies, waits for them, and re-layouts, on_device(): mode_block[:, None, 0:1] * mode_grad_x[None]  23.6 us
  transfers between devices with their start and end apart: 9, of which 3 were waited for; matrix products, arithmetic and copies ran while one was open for 4% of the time, Pallas kernels for 0%

commit v1 on v0

v1 whole, which is shorter than its diff:
```python
import math

import jax
import jax.numpy as jnp
from jax import lax
from jax.experimental import pallas as pl
from jax.experimental.pallas import tpu as pltpu
from jax.sharding import PartitionSpec as P

F32 = jnp.float32
BF16 = jnp.bfloat16
MESH = pl.DeviceIdType.MESH
HIGHEST = lax.Precision.HIGHEST

S = 48
R = 32768
CELLS = 2.0 * 64 * 4096
STEP = 0.25
VISCOUS = 0.2
ROWS, COLS, ALONG_X = 8, 32, 4
GROUP = ROWS * ALONG_X
DEEP = COLS // ALONG_X
CHUNK = 16
REGION = GROUP * CHUNK
PAIRS = 1176
WIDE = 1280
NT = (((1,), (1,)), ((), ()))


def split(value):
    high = value.astype(BF16)
    return high, (value - high.astype(F32)).astype(BF16)


def dot(a, b):
    return jnp.dot(a, b, preferred_element_type=F32)


def dot_nt(a, b):
    return lax.dot_general(a, b, NT, preferred_element_type=F32)


def exact(a, b):
    return jnp.dot(a, b, precision=HIGHEST, preferred_element_type=F32)


def exact_nt(a, b):
    return lax.dot_general(a, b, NT, precision=HIGHEST, preferred_element_type=F32)


def tall(value):
    return jnp.concatenate([value, jnp.zeros((128 - S, 128), F32)], axis=0)


def kernel(
    modes, mean, seeds, amps, water, new_modes, new_coeffs,
    base, both, grad_x, grad_y, back, weighted, pair_high, pair_low, side_high, side_low,
    square, coeffs, pair_coeffs, moments, tensor, cube, cube_split, pair_cov,
    cov_inv, gram_inv, half,
    part_a, deep_a, mine_a, total_a, part_b, deep_b, mine_b, total_b,
    up_out, down_out, left_out, right_out, up_in, down_in, left_in, right_in,
    up_out2, down_out2, left_out2, right_out2, up_in2, down_in2, left_in2, right_in2,
    halo_send, halo_recv, sum_send, sum_recv,
):
    row = lax.axis_index("row")
    col = lax.axis_index("col")
    along_x = lax.rem(col, ALONG_X)
    plane = lax.div(col, ALONG_X)
    place = row * ALONG_X + along_x
    above = lax.rem(row + ROWS - 1, ROWS)
    below = lax.rem(row + 1, ROWS)
    left = lax.rem(col + COLS - 1, COLS)
    right = lax.rem(col + 1, COLS)

    def member(offset):
        other = lax.rem(place + offset, GROUP)
        return other, (lax.div(other, ALONG_X), plane * ALONG_X + lax.rem(other, ALONG_X))

    def deep(offset):
        return (row, lax.rem(plane + offset, DEEP) * ALONG_X + along_x)

    barrier = pltpu.get_barrier_semaphore()

    def greet_plane(offset, carry):
        pl.semaphore_signal(barrier, inc=1, device_id=member(offset)[1], device_id_type=MESH)
        return carry

    def greet_deep(offset, carry):
        pl.semaphore_signal(barrier, inc=1, device_id=deep(offset), device_id_type=MESH)
        return carry

    lax.fori_loop(1, GROUP, greet_plane, 0)
    lax.fori_loop(1, DEEP, greet_deep, 0)
    pl.semaphore_signal(barrier, inc=1, device_id=(row, left), device_id_type=MESH)
    pl.semaphore_signal(barrier, inc=1, device_id=(row, right), device_id_type=MESH)

    lane = lax.broadcasted_iota(jnp.int32, (S, 128), 1)
    lane1 = lax.broadcasted_iota(jnp.int32, (1, 128), 1)
    sub = lax.broadcasted_iota(jnp.int32, (S, 128), 0)
    sub8 = lax.broadcasted_iota(jnp.int32, (8, 128), 0)

    def copies(outs, ins, first):
        targets = ((above, col), (below, col), (row, left), (row, right))
        arrivals = (ins[1], ins[0], ins[3], ins[2])
        return [
            pltpu.make_async_remote_copy(
                src_ref=outs[k],
                dst_ref=arrivals[k],
                send_sem=halo_send.at[first + k],
                recv_sem=halo_recv.at[first + k],
                device_id=targets[k],
                device_id_type=MESH,
            )
            for k in range(4)
        ]

    def plane_start(source, parts, sems):
        def send(offset, carry):
            other, device = member(offset)
            pltpu.make_async_remote_copy(
                src_ref=source.at[pl.ds(pl.multiple_of(other * CHUNK, CHUNK), CHUNK)],
                dst_ref=parts.at[pl.ds(pl.multiple_of((offset - 1) * CHUNK, CHUNK), CHUNK)],
                send_sem=sum_send.at[sems],
                recv_sem=sum_recv.at[sems],
                device_id=device,
                device_id_type=MESH,
            ).start()
            return carry

        lax.fori_loop(1, GROUP, send, 0)

    def deep_start(source, parts, mine, deeper, sems):
        pltpu.make_async_copy(parts, parts, sum_recv.at[sems]).wait()
        value = source[pl.ds(pl.multiple_of(place * CHUNK, CHUNK), CHUNK), :]
        for k in range(GROUP - 1):
            value = value + parts[k * CHUNK : (k + 1) * CHUNK, :]
        mine[0:CHUNK, :] = value

        def send(offset, carry):
            pltpu.make_async_remote_copy(
                src_ref=mine.at[pl.ds(0, CHUNK)],
                dst_ref=deeper.at[pl.ds(pl.multiple_of((offset - 1) * CHUNK, CHUNK), CHUNK)],
                send_sem=sum_send.at[sems + 1],
                recv_sem=sum_recv.at[sems + 1],
                device_id=deep(offset),
                device_id_type=MESH,
            ).start()
            return carry

        lax.fori_loop(1, DEEP, send, 0)

    def gather_start(mine, deeper, total, sems):
        pltpu.make_async_copy(deeper, deeper, sum_recv.at[sems + 1]).wait()
        value = mine[0:CHUNK, :]
        for k in range(DEEP - 1):
            value = value + deeper[k * CHUNK : (k + 1) * CHUNK, :]
        mine[CHUNK : 2 * CHUNK, :] = value
        own = pl.ds(pl.multiple_of(place * CHUNK, CHUNK), CHUNK)
        total[own, :] = value

        def send(offset, carry):
            pltpu.make_async_remote_copy(
                src_ref=mine.at[pl.ds(CHUNK, CHUNK)],
                dst_ref=total.at[own],
                send_sem=sum_send.at[sems + 2],
                recv_sem=sum_recv.at[sems + 2],
                device_id=member(offset)[1],
                device_id_type=MESH,
            ).start()
            return carry

        lax.fori_loop(1, GROUP, send, 0)

    def gather_wait(parts, sems):
        pltpu.make_async_copy(parts, parts, sum_recv.at[sems + 2]).wait()

    def sums_sent(parts, deeper, sems):
        pltpu.make_async_copy(parts, parts, sum_send.at[sems]).wait()
        pltpu.make_async_copy(deeper, deeper, sum_send.at[sems + 1]).wait()
        pltpu.make_async_copy(parts, parts, sum_send.at[sems + 2]).wait()

    side_high[...] = jnp.zeros((128, 2048), BF16)
    side_low[...] = jnp.zeros((128, 2048), BF16)
    first_column = jnp.zeros((56, 128), F32)
    last_column = jnp.zeros((56, 128), F32)
    lane56 = lax.broadcasted_iota(jnp.int32, (56, 128), 1)
    for t in range(16):
        s = t % 8
        cells = slice(t * 128, (t + 1) * 128)
        field = modes[pl.ds(t, S, stride=16), :]
        drift_row = jnp.where(sub8 == 0, jnp.broadcast_to(mean[t : t + 1, :], (8, 128)), 0.0)
        block = jnp.concatenate([field, drift_row], axis=0)
        base[t] = block
        both[t, 0:S, :] = field
        both[t, S : S + 24, :] = field[0:24]
        weight = water[s : s + 1, :].astype(F32) * (-1.0 / CELLS)
        high, low = split(field * weight)
        weighted[0:S, cells] = high
        weighted[S : 2 * S, cells] = low
        high, low = split(field)
        side_high[64 : 64 + S, cells] = high
        side_low[64 : 64 + S, cells] = low
        shifted = pltpu.roll(block, t, 1) if t else block
        first_column = jnp.where(lane56 == t, shifted, first_column)
        last_column = jnp.where(lane56 == t, pltpu.roll(block, t + 1, 1), last_column)
        if s == 0:
            up_out[t // 8] = block
        if s == 7:
            down_out[t // 8] = block
    left_out[...] = first_column
    right_out[...] = last_column

    pl.semaphore_wait(barrier, GROUP - 1 + DEEP - 1 + 2)
    halo = copies(
        (up_out, down_out, left_out, right_out), (up_in, down_in, left_in, right_in), 0
    )
    for copy in halo:
        copy.start()

    phase = seeds[...].astype(F32) * (3.0 * math.pi / 8192.0)
    wave = jnp.cos(phase)
    number = (row * COLS + col) * 128 + lax.broadcasted_iota(jnp.int32, (128, S), 0)
    strength = 0.5 + number.astype(F32) * (1.0 / R)
    square[...] = jnp.zeros((128, 128), F32)
    square[:, 0:S] = strength * amps[...] * (wave + (wave * wave - 0.5))
    raw = square[...].T[0:S]

    def pair_up(values, ones):
        coeffs[0:S, :] = values
        coeffs[S : S + 24, :] = values[0:24]
        for d in range(24):
            pair_coeffs[d * S : (d + 1) * S, :] = values * coeffs[d : d + S, :]
        pair_coeffs[1152:PAIRS, :] = values[0:24] * coeffs[24:48, :]
        pair_coeffs[PAIRS : PAIRS + S, :] = values
        pair_coeffs[PAIRS + S : WIDE, :] = jnp.zeros((WIDE - PAIRS - S, 128), F32)
        if ones:
            pair_coeffs[1272:1280, :] = jnp.where(sub8 == 0, 1.0, 0.0)

    pair_up(raw, True)
    for lb in range(5):
        out = exact_nt(raw, pair_coeffs[lb * 256 : (lb + 1) * 256, :])
        moments[lb * 96 : lb * 96 + S, :] = out[:, 0:128]
        moments[lb * 96 + S : lb * 96 + 96, :] = out[:, 128:256]
    gram = dot_nt(weighted[...], side_high[...])
    gram = gram[0:S] + gram[S : 2 * S] + dot_nt(weighted[0:S, :], side_low[...])
    moments[432:480, :] = moments[432:480, :] - pltpu.roll(gram, 8, 1)
    moments[480:REGION, :] = jnp.zeros((REGION - 480, 128), F32)
    plane_start(moments, part_a, 0)

    for copy in halo:
        copy.wait_recv()
    first_row = row == 0
    last_row = row == ROWS - 1
    from_left = jnp.where(col == 0, 0.0, left_in[...])
    from_right = jnp.where(col == COLS - 1, 0.0, right_in[...])
    for t in range(16):
        c, s = divmod(t, 8)
        block = base[t]
        if s == 0:
            before = jnp.where(first_row, 0.0, up_in[c])
        else:
            before = base[t - 1]
        if s == 7:
            after = jnp.where(last_row, 0.0, down_in[c])
        else:
            after = base[t + 1]
        along = 0.5 * (after - before)
        ahead = jnp.where(lane56 == 127, pltpu.roll(from_right, 127 - t, 1), pltpu.roll(block, 127, 1))
        shifted = pltpu.roll(from_left, 128 - t, 1) if t else from_left
        behind = jnp.where(lane56 == 0, shifted, pltpu.roll(block, 1, 1))
        across = 0.5 * (ahead - behind)
        grad_x[t, 0:S, :] = along[0:S]
        grad_x[t, S : S + 24, :] = along[0:24]
        grad_x[t, 72:80, :] = along[S:56]
        grad_y[t, 0:S, :] = across[0:S]
        grad_y[t, S : S + 24, :] = across[0:24]
        grad_y[t, 72:80, :] = across[S:56]

    def pair_value(d, s, c, u0, u1, v0, v1):
        t = c * 8 + s
        ahead = pl.ds(d, S)
        return (
            u0 * grad_x[t, ahead, :] + u1 * grad_y[t, ahead, :]
            + v0 * grad_x[t, 0:S, :] + v1 * grad_y[t, 0:S, :]
        )

    def pair_block(d, carry):
        rows = pl.ds(pl.multiple_of(d * S, S), S)
        for s in range(8):
            u0, u1 = both[s, 0:S, :], both[8 + s, 0:S, :]
            v0, v1 = both[s, pl.ds(d, S), :], both[8 + s, pl.ds(d, S), :]
            for c in range(2):
                t = c * 8 + s
                high, low = split(pair_value(d, s, c, u0, u1, v0, v1))
                pair_high[rows, t * 128 : (t + 1) * 128] = high
                pair_low[rows, t * 128 : (t + 1) * 128] = low
        return carry

    for s in range(8):
        u0, u1 = both[s, 0:S, :], both[8 + s, 0:S, :]
        v0, v1 = both[s, 24:72, :], both[8 + s, 24:72, :]
        m0, m1 = base[s, S : S + 1, :], base[8 + s, S : S + 1, :]
        for c in range(2):
            t = c * 8 + s
            cells = slice(t * 128, (t + 1) * 128)
            value = u0 * grad_x[t, 0:S, :] + u1 * grad_y[t, 0:S, :]
            high, low = split(value)
            pair_high[0:S, cells] = high
            pair_low[0:S, cells] = low
            value = pair_value(24, s, c, u0, u1, v0, v1)
            minus = (
                m0 * grad_x[t, 0:S, :] + m1 * grad_y[t, 0:S, :]
                + u0 * grad_x[t, 72:73, :] + u1 * grad_y[t, 72:73, :]
            )
            back[t] = minus
            high, low = split(jnp.concatenate([value[0:24], minus[0:24]], axis=0))
            pair_high[1152:1200, cells] = high
            pair_low[1152:1200, cells] = low
            high, low = split(jnp.concatenate([minus[24:48], jnp.zeros((56, 128), F32)], axis=0))
            pair_high[1200:1280, cells] = high
            pair_low[1200:1280, cells] = low
    lax.fori_loop(1, 12, pair_block, 0)
    deep_start(moments, part_a, mine_a, deep_a, 0)
    lax.fori_loop(12, 24, pair_block, 0)
    gather_start(mine_a, deep_a, total_a, 0)

    def project(lb, carry):
        rows = pl.ds(pl.multiple_of(lb * 256, 256), 256)
        high = pair_high[rows, :]
        out = dot_nt(weighted[...], high)
        out = out[0:S] + out[S : 2 * S] + dot_nt(weighted[0:S, :], pair_low[rows, :])
        tensor[pl.ds(pl.multiple_of(lb * 96, 96), S), :] = out[:, 0:128]
        tensor[pl.ds(pl.multiple_of(lb * 96 + S, S), S), :] = out[:, 128:256]
        return carry

    lax.fori_loop(0, 5, project, 0)
    tensor[480:REGION, :] = jnp.zeros((REGION - 480, 128), F32)
    plane_start(tensor, part_b, 3)

    gather_wait(part_a, 0)
    tail = total_a[432:480, :]
    second = jnp.where(lane < S, pltpu.roll(tail, 128 - 24, 1), 0.0) * (1.0 / R)
    gram_inv[...] = jnp.where(lane < S, pltpu.roll(tail, 128 - 72, 1), 0.0)
    mean_col = jnp.sum(jnp.where(lane == 120, tail, 0.0), axis=1, keepdims=True) * (1.0 / R)
    mean_row = jnp.sum(jnp.where(lane == sub, mean_col, 0.0), axis=0, keepdims=True)
    cov_inv[...] = second - mean_col * mean_row
    for lb in range(10):
        number = lb * 128 + lane
        first_d = lb * 128 // S
        d = jnp.full((S, 128), first_d, jnp.int32)
        for step in range(first_d + 1, first_d + 4):
            d = d + jnp.where(number >= step * S, 1, 0)
        k = number - d * S
        l = k + d
        l = jnp.where(l >= S, l - S, l)
        hot_k = jnp.where(sub == k, 1.0, 0.0)
        hot_l = jnp.where(sub == l, 1.0, 0.0)
        at_k = exact(second, tall(hot_k))
        at_l = exact(second, tall(hot_l))
        mean_k = jnp.sum(mean_col * hot_k, axis=0, keepdims=True)
        mean_l = jnp.sum(mean_col * hot_l, axis=0, keepdims=True)
        second_kl = jnp.sum(hot_k * at_l, axis=0, keepdims=True)
        third = total_a[lb * S : (lb + 1) * S, :] * (1.0 / R)
        third = third - mean_col * (second_kl - 2.0 * (mean_k * mean_l)) - mean_k * at_l - mean_l * at_k
        cov = second_kl - mean_k * mean_l
        if lb == 9:
            third = jnp.where(lane < 24, third, 0.0)
            cov = jnp.where(lane1 < 24, cov, 0.0)
        cube[lb * S : (lb + 1) * S, :] = third
        high, low = split(third)
        cube_split[0:S, lb * 128 : (lb + 1) * 128] = high
        cube_split[S : 2 * S, lb * 128 : (lb + 1) * 128] = low
        pair_cov[lb : lb + 1, :] = cov

    def contract(n, carry):
        cells = pl.ds(pl.multiple_of(n * 256, 256), 256)
        out = dot(cube_split[...], pair_high[:, cells])
        out = out[0:S] + out[S : 2 * S] + dot(cube_split[0:S, :], pair_low[:, cells])
        high, low = split(out)
        side_high[0:S, cells] = high
        side_low[0:S, cells] = low
        return carry

    lax.fori_loop(0, 8, contract, 0)
    deep_start(tensor, part_b, mine_b, deep_b, 3)

    def eliminate(i, carry):
        for matrix in (cov_inv, gram_inv):
            value = matrix[...]
            line = matrix[pl.ds(i, 1), :]
            pivot = jnp.sum(jnp.where(lane1 == i, line, 0.0), axis=1, keepdims=True)
            column = jnp.sum(jnp.where(lane == i, value, 0.0), axis=1, keepdims=True)
            inverse = 1.0 / pivot
            line = jnp.where(lane1 == i, inverse, line * inverse)
            value = jnp.where(lane == i, 0.0, value) - column * line
            matrix[...] = jnp.where(sub == i, line, value)
        return carry

    lax.fori_loop(0, S, eliminate, 0)
    gather_start(mine_b, deep_b, total_b, 3)
    centred = raw - mean_col
    pair_up(centred, False)
    gather_wait(part_b, 3)

    cross = jnp.zeros((S, 128), F32)
    for lb in range(10):
        rows = slice(lb * S, (lb + 1) * S)
        cross = cross + exact_nt(total_b[rows, :], tall(cube[rows, :]))
    lin_proj = jnp.where(lane < S, pltpu.roll(total_b[432:480, :], 128 - 24, 1), 0.0)
    projected = lin_proj + exact(cross, tall(cov_inv[...]))
    solved = exact(gram_inv[...], tall(projected))
    unit = jnp.where(lane == sub, 1.0, 0.0)
    turned = exact_nt(unit, tall(solved))
    factors = jnp.where(lane < S, cov_inv[...], pltpu.roll(turned, 64, 1))
    high, low = split(factors)
    lowest = (factors - high.astype(F32) - low.astype(F32)).astype(BF16)
    factors = jnp.concatenate([high, low, lowest], axis=0)
    first_column = jnp.zeros((S, 128), F32)
    last_column = jnp.zeros((S, 128), F32)
    for n in range(8):
        cells = slice(n * 256, (n + 1) * 256)
        out = dot(factors, side_high[:, cells])
        rest = dot(factors[0 : 2 * S], side_low[:, cells])
        out = out[0:S] + out[S : 2 * S] + out[2 * S : 3 * S] + rest[0:S] + rest[S : 2 * S]
        for t in (2 * n, 2 * n + 1):
            c, s = divmod(t, 8)
            part = out[:, 0:128] if t % 2 == 0 else out[:, 128:256]
            mask = water[s : s + 1, :].astype(F32)
            value = mask * (both[t, 0:S, :] - STEP * (back[t] + part))
            half[t] = value
            shifted = pltpu.roll(value, t, 1) if t else value
            first_column = jnp.where(lane == t, shifted, first_column)
            last_column = jnp.where(lane == t, pltpu.roll(value, t + 1, 1), last_column)
            if s == 0:
                up_out2[c] = value
            if s == 7:
                down_out2[c] = value
    left_out2[...] = first_column
    right_out2[...] = last_column
    halo2 = copies(
        (up_out2, down_out2, left_out2, right_out2), (up_in2, down_in2, left_in2, right_in2), 4
    )
    for copy in halo2:
        copy.start()

    change = jnp.zeros((S, 128), F32)
    excess = jnp.zeros((S, 128), F32)
    for lb in range(10):
        here = total_b[lb * S : (lb + 1) * S, :]
        change = change + exact(here, pair_coeffs[lb * 128 : (lb + 1) * 128, :])
        excess = excess + here * pair_cov[lb : lb + 1, :]
    change = change - jnp.sum(excess, axis=1, keepdims=True)
    square[0:S, :] = centred + STEP * exact(gram_inv[...], tall(change))
    new_coeffs[...] = square[...].T[:, 0:S]

    for copy in halo2:
        copy.wait_recv()
    from_left = jnp.where(col == 0, 0.0, left_in2[...])
    from_right = jnp.where(col == COLS - 1, 0.0, right_in2[...])
    for t in range(16):
        c, s = divmod(t, 8)
        value = half[t]
        before = jnp.where(first_row, 0.0, up_in2[c]) if s == 0 else half[t - 1]
        after = jnp.where(last_row, 0.0, down_in2[c]) if s == 7 else half[t + 1]
        ahead = jnp.where(lane == 127, pltpu.roll(from_right, 127 - t, 1), pltpu.roll(value, 127, 1))
        shifted = pltpu.roll(from_left, 128 - t, 1) if t else from_left
        behind = jnp.where(lane == 0, shifted, pltpu.roll(value, 1, 1))
        laplace = after + before + ahead + behind - 4.0 * value
        mask = water[s : s + 1, :].astype(F32)
        new_modes[pl.ds(t, S, stride=16), :] = mask * (value + VISCOUS * laplace)

    for copy in halo + halo2:
        copy.wait_send()
    sums_sent(part_a, deep_a, 0)
    sums_sent(part_b, deep_b, 3)


def on_device(modes, mean_flow, seeds, amplitudes, water_mask):
    vmem = pl.BlockSpec(memory_space=pltpu.VMEM)

    def f32(*shape):
        return pltpu.VMEM(shape, F32)

    def bf16(*shape):
        return pltpu.VMEM(shape, BF16)

    sums = [
        f32((GROUP - 1) * CHUNK, 128), f32((DEEP - 1) * CHUNK, 128), f32(2 * CHUNK, 128), f32(REGION, 128)
    ]
    new_modes, new_coeffs = pl.pallas_call(
        kernel,
        out_shape=(
            jax.ShapeDtypeStruct((S * 16, 128), F32),
            jax.ShapeDtypeStruct((128, S), F32),
        ),
        in_specs=[vmem] * 5,
        out_specs=(vmem, vmem),
        scratch_shapes=[
            f32(16, 56, 128), f32(16, 72, 128), f32(16, 80, 128), f32(16, 80, 128), f32(16, S, 128),
            bf16(2 * S, 2048), bf16(WIDE, 2048), bf16(WIDE, 2048), bf16(128, 2048), bf16(128, 2048),
            f32(128, 128), f32(72, 128), f32(WIDE, 128),
            f32(REGION, 128), f32(REGION, 128), f32(480, 128), bf16(2 * S, WIDE),
            f32(16, 128), f32(S, 128), f32(S, 128), f32(16, S, 128),
            *sums, *sums,
            *([f32(2, 56, 128)] * 2 + [f32(56, 128)] * 2) * 2,
            *([f32(2, S, 128)] * 2 + [f32(S, 128)] * 2) * 2,
            pltpu.SemaphoreType.DMA((8,)), pltpu.SemaphoreType.DMA((8,)),
            pltpu.SemaphoreType.DMA((6,)), pltpu.SemaphoreType.DMA((6,)),
        ],
        compiler_params=pltpu.CompilerParams(
            collective_id=0, has_side_effects=True, vmem_limit_bytes=56 * 1024 * 1024
        ),
    )(
        modes.reshape(S * 16, 128),
        mean_flow.reshape(16, 128),
        seeds,
        amplitudes.reshape(1, S),
        water_mask,
    )
    return new_modes.reshape(S, 2, 8, 128), new_coeffs


def solution(mesh):
    return jax.shard_map(
        on_device,
        mesh=mesh,
        in_specs=(
            P(None, None, "row", "col"),
            P(None, "row", "col"),
            P(("row", "col"), None),
            P(),
            P("row", "col"),
        ),
        out_specs=(P(None, None, "row", "col"), P(("row", "col"), None)),
        check_vma=False,
    )
```

time: 688 us -> 57.3 us (0.08); the launches traced: 677 us -> 57.1 us
  waiting for transfers between devices: 255 us -> 0 us
  blocking collectives: 230 us -> 0 us
  matrix products: 63.3 us -> 0 us
  Pallas kernels: 0 us -> 51.7 us
  local copies, waits for them, and re-layouts: 55.7 us -> 4.76 us
  other arithmetic: 34.8 us -> 0 us
  starting transfers between devices: 23.2 us -> 0 us
  between operations: 15 us -> 0.64 us
    psum x1 -> x0, waiting for transfers between devices: 245 us -> none  [on_device(): second, third_sum = lax.psum((local_second, local_third), ('row', 'col'))]
    psum x3 -> x0, blocking collectives: 230 us -> none  [the longest x1 78.6 us: on_device(): column_sum = lax.psum(jnp.sum(uncentered, axis=0), ('row', 'col'))]
    dot_general x20 -> x0, matrix products: 54.7 us -> none  [the longest x9 29.6 us: matmul_nt(): lax.dot_general(left_side, right_side, (((1,), (1,)), ((), ())), precisio...]
    pallas_call x0 -> x1, Pallas kernels: none -> 51.7 us  [on_device(): pl.pallas_call(kernel, out_shape=(jax.ShapeDtypeStruct((S * 16, 128), F32...]
    add x6 -> x0, local copies, waits for them, and re-layouts: 23.6 us -> none  [on_device(): mode_block[:, None, 0:1] * mode_grad_x[None]]
    ppermute x8 -> x0, starting transfers between devices: 23.2 us -> none  [the longest x4 12.6 us: with_halo(): lax.ppermute(tail, axis, [(i, (i + 1) % count) for i in range(ends)])]
    another operation x11 -> x0, other arithmetic: 23.2 us -> none  [the longest x4 11.3 us: factor_solve(): lax.linalg.triangular_solve(factor, lower_part, left_side=True, lower=Tru...]
    slice x16 -> x0, local copies, waits for them, and re-layouts: 10.4 us -> none  [the longest x7 9.12 us: on_device(): weight_cube[:, offset:offset + BLOCK_MODES, :].reshape(mode_count, -1)]
  transfers between devices with their start and end apart: 9 -> 0, of which waited for: 3 -> 0; matrix products, arithmetic and copies ran while one was open for 4% -> 0% of each run, Pallas kernels for 0% -> 0%
where the time goes in v1:
time: 57.3 us; the launch traced here: 57.1 us
  Pallas kernels  51.7 us (90%)
  local copies, waits for them, and re-layouts  4.76 us (8%)
  between operations  0.64 us (1%)
    pallas_call x1, Pallas kernels, on_device(): pl.pallas_call(kernel, out_shape=(jax.ShapeDtypeStruct((S * 16, 128), F32...  51.7 us
    unnamed x3, local copies, waits for them, and re-layouts  4.76 us

profile of v1, /device:TPU:1, one launch (start us, length us, event | category | flops | bytes accessed | tf_op | source)
XLA Modules:
  0.0 57.1 jit_solution(4543150017312887223)
XLA Ops:
  0.6 1.5 %copy.7.seeds = s32[128,48]{1,0:T(8,128)} copy(s32[128,48]{0,1:T(8,128)} %param.7) | data formatting | bytes 49152 | tf_op args[2]
  2.1 51.7 %shard_map.68 = (f32[768,128]{1,0:T(8,128)}, f32[128,48]{1,0:T(8,128)}) custom-call(f32[768,128]{1,0:T(8,128)} %bitcast.5, f32[16,128]{1,0:T(8,128)} %bitcast.6, s32[128,48]{1,0:T(8,128)} %copy.7.seeds, f32[1,48]{1,0:T(1,128)} %bitcast.7, s32[8,128]{1,0:T(8,128)} %water.1), custom_call_target="tpu_custom_call" | custom-call | tf_op jit(solution)/shard_map/pallas_call | solution.py:490
  53.8 1.5 %copy.8 = f32[128,48]{0,1:T(8,128)} copy(f32[128,48]{1,0:T(8,128)} %get-tuple-element.7) | data formatting | bytes 49152
  55.3 1.8 %copy.10 = f32[48,2,8,128]{3,2,1,0:T(8,128)} copy(f32[48,2,8,128]{3,2,1,0:T(8,128)} %bitcast.4) | data formatting | bytes 786432

commit v2 on v1

v2 whole, which is shorter than its diff:
```python
import math

import jax
import jax.numpy as jnp
from jax import lax
from jax.experimental import pallas as pl
from jax.experimental.pallas import tpu as pltpu
from jax.sharding import PartitionSpec as P

F32 = jnp.float32
BF16 = jnp.bfloat16
MESH = pl.DeviceIdType.MESH
HIGHEST = lax.Precision.HIGHEST

S = 48
R = 32768
CELLS = 2.0 * 64 * 4096
STEP = 0.25
VISCOUS = 0.2
ROWS, COLS, ALONG_X = 8, 32, 4
GROUP = ROWS * ALONG_X
DEEP = COLS // ALONG_X
CHUNK = 16
REGION = GROUP * CHUNK
PAIRS = 1176
WIDE = 1280
INNER = [(c, s) for s in range(1, 7) for c in range(2)]
OUTER = [(c, s) for s in (0, 7) for c in range(2)]
SLOT = {place: number for number, place in enumerate(INNER + OUTER)}
SEAM = 16
LANES = 18 * 128
INNER_LANES = 12 * 128
NT = (((1,), (1,)), ((), ()))


def split(value):
    high = value.astype(BF16)
    return high, (value - high.astype(F32)).astype(BF16)


def dot(a, b):
    return jnp.dot(a, b, preferred_element_type=F32)


def dot_nt(a, b):
    return lax.dot_general(a, b, NT, preferred_element_type=F32)


def exact(a, b):
    return jnp.dot(a, b, precision=HIGHEST, preferred_element_type=F32)


def exact_nt(a, b):
    return lax.dot_general(a, b, NT, precision=HIGHEST, preferred_element_type=F32)


def tall(value):
    return jnp.concatenate([value, jnp.zeros((128 - S, 128), F32)], axis=0)


def kernel(
    modes_hbm, mean_hbm, seeds_hbm, amps_hbm, water_hbm, new_modes, new_coeffs,
    modes, mean, seeds, amps, water,
    base, both, grad_x, grad_y, back, weighted, pair_high, pair_low, side_high, side_low,
    seam_field, seam_slope, seam_back, amp_row, coeffs, pair_coeffs, moments, tensor, cube, cube_split, pair_cov,
    cov_inv, gram_inv, half, key_high, key_low,
    part_a, deep_a, mine_a, total_a, part_b, deep_b, mine_b, total_b,
    up_out, down_out, side_out, up_in, down_in, left_in, right_in,
    up_out2, down_out2, side_out2, up_in2, down_in2, left_in2, right_in2,
    halo_send, halo_recv, sum_send, sum_recv, fetch_sem,
):
    row = lax.axis_index("row")
    col = lax.axis_index("col")
    along_x = lax.rem(col, ALONG_X)
    plane = lax.div(col, ALONG_X)
    place = row * ALONG_X + along_x
    above = lax.rem(row + ROWS - 1, ROWS)
    below = lax.rem(row + 1, ROWS)
    left = lax.rem(col + COLS - 1, COLS)
    right = lax.rem(col + 1, COLS)

    def member(offset):
        other = lax.rem(place + offset, GROUP)
        return other, (lax.div(other, ALONG_X), plane * ALONG_X + lax.rem(other, ALONG_X))

    def deep(offset):
        return (row, lax.rem(plane + offset, DEEP) * ALONG_X + along_x)

    barrier = pltpu.get_barrier_semaphore()

    def greet_plane(offset, carry):
        pl.semaphore_signal(barrier, inc=1, device_id=member(offset)[1], device_id_type=MESH)
        return carry

    def greet_deep(offset, carry):
        pl.semaphore_signal(barrier, inc=1, device_id=deep(offset), device_id_type=MESH)
        return carry

    lax.fori_loop(1, GROUP, greet_plane, 0)
    lax.fori_loop(1, DEEP, greet_deep, 0)
    pl.semaphore_signal(barrier, inc=1, device_id=(row, left), device_id_type=MESH)
    pl.semaphore_signal(barrier, inc=1, device_id=(row, right), device_id_type=MESH)

    fetches = [
        pltpu.make_async_copy(source, target, fetch_sem.at[k])
        for k, (source, target) in enumerate(
            ((seeds_hbm, seeds), (amps_hbm, amps), (modes_hbm, modes), (mean_hbm, mean), (water_hbm, water))
        )
    ]
    for fetch in fetches:
        fetch.start()

    lane = lax.broadcasted_iota(jnp.int32, (S, 128), 1)
    lane1 = lax.broadcasted_iota(jnp.int32, (1, 128), 1)
    sub = lax.broadcasted_iota(jnp.int32, (S, 128), 0)
    sub8 = lax.broadcasted_iota(jnp.int32, (8, 128), 0)

    def copies(outs, ins, first):
        targets = ((above, col), (below, col), (row, left), (row, right))
        arrivals = (ins[1], ins[0], ins[3], ins[2])
        return [
            pltpu.make_async_remote_copy(
                src_ref=outs[k],
                dst_ref=arrivals[k],
                send_sem=halo_send.at[first + k],
                recv_sem=halo_recv.at[first + k],
                device_id=targets[k],
                device_id_type=MESH,
            )
            for k in range(4)
        ]

    def plane_start(source, parts, sems):
        def send(offset, carry):
            other, device = member(offset)
            pltpu.make_async_remote_copy(
                src_ref=source.at[pl.ds(pl.multiple_of(other * CHUNK, CHUNK), CHUNK)],
                dst_ref=parts.at[pl.ds(pl.multiple_of((offset - 1) * CHUNK, CHUNK), CHUNK)],
                send_sem=sum_send.at[sems],
                recv_sem=sum_recv.at[sems],
                device_id=device,
                device_id_type=MESH,
            ).start()
            return carry

        lax.fori_loop(1, GROUP, send, 0)

    def deep_start(source, parts, mine, deeper, sems):
        pltpu.make_async_copy(parts, parts, sum_recv.at[sems]).wait()
        value = source[pl.ds(pl.multiple_of(place * CHUNK, CHUNK), CHUNK), :]
        for k in range(GROUP - 1):
            value = value + parts[k * CHUNK : (k + 1) * CHUNK, :]
        mine[0:CHUNK, :] = value

        def send(offset, carry):
            pltpu.make_async_remote_copy(
                src_ref=mine.at[pl.ds(0, CHUNK)],
                dst_ref=deeper.at[pl.ds(pl.multiple_of((offset - 1) * CHUNK, CHUNK), CHUNK)],
                send_sem=sum_send.at[sems + 1],
                recv_sem=sum_recv.at[sems + 1],
                device_id=deep(offset),
                device_id_type=MESH,
            ).start()
            return carry

        lax.fori_loop(1, DEEP, send, 0)

    def gather_start(mine, deeper, total, sems):
        pltpu.make_async_copy(deeper, deeper, sum_recv.at[sems + 1]).wait()
        value = mine[0:CHUNK, :]
        for k in range(DEEP - 1):
            value = value + deeper[k * CHUNK : (k + 1) * CHUNK, :]
        mine[CHUNK : 2 * CHUNK, :] = value
        own = pl.ds(pl.multiple_of(place * CHUNK, CHUNK), CHUNK)
        total[own, :] = value

        def send(offset, carry):
            pltpu.make_async_remote_copy(
                src_ref=mine.at[pl.ds(CHUNK, CHUNK)],
                dst_ref=total.at[own],
                send_sem=sum_send.at[sems + 2],
                recv_sem=sum_recv.at[sems + 2],
                device_id=member(offset)[1],
                device_id_type=MESH,
            ).start()
            return carry

        lax.fori_loop(1, GROUP, send, 0)

    def gather_wait(parts, sems):
        pltpu.make_async_copy(parts, parts, sum_recv.at[sems + 2]).wait()

    def sums_sent(parts, deeper, sems):
        pltpu.make_async_copy(parts, parts, sum_send.at[sems]).wait()
        pltpu.make_async_copy(deeper, deeper, sum_send.at[sems + 1]).wait()
        pltpu.make_async_copy(parts, parts, sum_send.at[sems + 2]).wait()

    for fetch in fetches[:2]:
        fetch.wait()
    phase = seeds[...].astype(F32) * (3.0 * math.pi / 8192.0)
    wave = jnp.cos(phase)
    strength = 0.5 + ((row * COLS + col) * 128 + lane).astype(F32) * (1.0 / R)
    amp_row[...] = jnp.zeros((8, 128), F32)
    amp_row[0:1, 0:S] = amps[...]
    amp_col = jnp.sum(jnp.where(lane == sub, amp_row[0:1, :], 0.0), axis=1, keepdims=True)
    raw = strength * amp_col * (wave + (wave * wave - 0.5))

    def pair_up(values, ones):
        coeffs[0:S, :] = values
        coeffs[S : S + 24, :] = values[0:24]
        for d in range(24):
            pair_coeffs[d * S : (d + 1) * S, :] = values * coeffs[d : d + S, :]
        pair_coeffs[1152:PAIRS, :] = values[0:24] * coeffs[24:48, :]
        pair_coeffs[PAIRS : PAIRS + S, :] = values
        pair_coeffs[PAIRS + S : WIDE, :] = jnp.zeros((WIDE - PAIRS - S, 128), F32)
        if ones:
            pair_coeffs[1272:1280, :] = jnp.where(sub8 == 0, 1.0, 0.0)

    pair_up(raw, True)
    for lb in range(5):
        out = exact_nt(raw, pair_coeffs[lb * 256 : (lb + 1) * 256, :])
        moments[lb * 96 : lb * 96 + S, :] = out[:, 0:128]
        moments[lb * 96 + S : lb * 96 + 96, :] = out[:, 128:256]
    for fetch in fetches[2:]:
        fetch.wait()

    def lanes_of(c, s):
        return slice(SLOT[c, s] * 128, (SLOT[c, s] + 1) * 128)

    seam_lanes = slice(SEAM * 128, LANES)
    side_high[...] = jnp.zeros((128, LANES), BF16)
    side_low[...] = jnp.zeros((128, LANES), BF16)
    lane56 = lax.broadcasted_iota(jnp.int32, (56, 128), 1)
    columns = jnp.zeros((56, 128), F32)
    shore = jnp.zeros((1, 128), F32)
    for t in range(16):
        c, s = divmod(t, 8)
        field = modes[pl.ds(t, S, stride=16), :]
        drift_row = jnp.where(sub8 == 0, jnp.broadcast_to(mean[t : t + 1, :], (8, 128)), 0.0)
        block = jnp.concatenate([field, drift_row], axis=0)
        base[t] = block
        both[t, 0:S, :] = field
        both[t, S : S + 24, :] = field[0:24]
        weight = water[s : s + 1, :].astype(F32) * (-1.0 / CELLS)
        high, low = split(field * weight)
        weighted[0:S, lanes_of(c, s)] = high
        weighted[S : 2 * S, lanes_of(c, s)] = low
        high, low = split(field)
        side_high[64 : 64 + S, lanes_of(c, s)] = high
        side_low[64 : 64 + S, lanes_of(c, s)] = low
        columns = jnp.where(lane56 == 64 + t, pltpu.roll(block, 64 + t, 1), columns)
        columns = jnp.where(lane56 == t, pltpu.roll(block, t + 1, 1), columns)
        shore = jnp.where(lane1 == t, pltpu.roll(weight, t, 1) if t else weight, shore)
        shore = jnp.where(lane1 == 64 + t, pltpu.roll(weight, 65 + t, 1), shore)
        if s == 0:
            up_out[c] = block
        if s == 7:
            down_out[c] = block
        ahead = jnp.where(lane56 == 127, 0.0, pltpu.roll(block, 127, 1))
        behind = jnp.where(lane56 == 0, 0.0, pltpu.roll(block, 1, 1))
        across = 0.5 * (ahead - behind)
        grad_y[t, 0:S, :] = across[0:S]
        grad_y[t, S : S + 24, :] = across[0:24]
        grad_y[t, 72:80, :] = across[S:56]
    side_out[...] = columns

    def slope(t, before, after):
        along = 0.5 * (after - before)
        grad_x[t, 0:S, :] = along[0:S]
        grad_x[t, S : S + 24, :] = along[0:24]
        grad_x[t, 72:80, :] = along[S:56]

    for c, s in INNER:
        slope(c * 8 + s, base[c * 8 + s - 1], base[c * 8 + s + 1])

    own = pltpu.roll(columns, 64, 1)
    high, low = split(own[0:S] * shore)
    weighted[0:S, seam_lanes] = jnp.concatenate([high, jnp.zeros((S, 128), BF16)], axis=1)
    weighted[S : 2 * S, seam_lanes] = jnp.concatenate([low, jnp.zeros((S, 128), BF16)], axis=1)
    second_half = lax.rem(lax.div(lane56, 8), 2) == 1
    own = jnp.where(second_half, own, pltpu.roll(own, 120, 1))
    seam_field[0:S, :] = own[0:S]
    seam_field[S : S + 24, :] = own[0:24]
    seam_field[72:80, :] = own[S:56]

    gram = dot_nt(weighted[...], side_high[...])
    gram = gram[0:S] + gram[S : 2 * S] + dot_nt(weighted[0:S, :], side_low[...])
    moments[432:480, :] = moments[432:480, :] - pltpu.roll(gram, 8, 1)
    moments[480:REGION, :] = jnp.zeros((REGION - 480, 128), F32)
    pl.semaphore_wait(barrier, GROUP - 1 + DEEP - 1 + 2)
    halo = copies(
        (up_out, down_out, side_out, side_out), (up_in, down_in, left_in, right_in), 0
    )
    for copy in halo:
        copy.start()
    plane_start(moments, part_a, 0)

    def pair_value(d, t, u0, u1, v0, v1):
        ahead = pl.ds(d, S)
        return (
            u0 * grad_x[t, ahead, :] + u1 * grad_y[t, ahead, :]
            + v0 * grad_x[t, 0:S, :] + v1 * grad_y[t, 0:S, :]
        )

    def store(rows, lanes, value):
        high, low = split(value)
        pair_high[rows, lanes] = high
        pair_low[rows, lanes] = low

    def pairs_of(grid_rows):
        def pair_block(d, carry):
            rows = pl.ds(pl.multiple_of(d * S, S), S)
            for s in grid_rows:
                u0, u1 = both[s, 0:S, :], both[8 + s, 0:S, :]
                v0, v1 = both[s, pl.ds(d, S), :], both[8 + s, pl.ds(d, S), :]
                for c in range(2):
                    store(rows, lanes_of(c, s), pair_value(d, c * 8 + s, u0, u1, v0, v1))
            return carry

        return pair_block

    def last_rows(lanes, value, minus):
        store(slice(1152, 1200), lanes, jnp.concatenate([value[0:24], minus[0:24]], axis=0))
        store(slice(1200, WIDE), lanes, jnp.concatenate([minus[24:48], jnp.zeros((56, 128), F32)], axis=0))

    def other_pairs(grid_rows):
        for s in grid_rows:
            u0, u1 = both[s, 0:S, :], both[8 + s, 0:S, :]
            v0, v1 = both[s, 24:72, :], both[8 + s, 24:72, :]
            m0, m1 = base[s, S : S + 1, :], base[8 + s, S : S + 1, :]
            for c in range(2):
                t = c * 8 + s
                store(slice(0, S), lanes_of(c, s), u0 * grad_x[t, 0:S, :] + u1 * grad_y[t, 0:S, :])
                minus = (
                    m0 * grad_x[t, 0:S, :] + m1 * grad_y[t, 0:S, :]
                    + u0 * grad_x[t, 72:73, :] + u1 * grad_y[t, 72:73, :]
                )
                back[t] = minus
                last_rows(lanes_of(c, s), pair_value(24, t, u0, u1, v0, v1), minus)

    def project_of(lanes, add):
        def project(lb, carry):
            rows = pl.ds(pl.multiple_of(lb * 256, 256), 256)
            out = dot_nt(weighted[:, lanes], pair_high[rows, lanes])
            out = out[0:S] + out[S : 2 * S] + dot_nt(weighted[0:S, lanes], pair_low[rows, lanes])
            for k in range(2):
                to = pl.ds(pl.multiple_of(lb * 96 + k * S, S), S)
                part = out[:, k * 128 : (k + 1) * 128]
                tensor[to, :] = tensor[to, :] + part if add else part
            return carry

        return project

    other_pairs(range(1, 7))
    lax.fori_loop(1, 24, pairs_of(range(1, 7)), 0)
    lax.fori_loop(0, 5, project_of(slice(0, INNER_LANES), False), 0)

    for copy in halo:
        copy.wait_recv()
    for c in range(2):
        slope(c * 8, jnp.where(row == 0, 0.0, up_in[c]), base[c * 8 + 1])
        slope(c * 8 + 7, base[c * 8 + 6], jnp.where(row == ROWS - 1, 0.0, down_in[c]))
    from_left = jnp.where(col == 0, 0.0, left_in[...])
    from_right = jnp.where(col == COLS - 1, 0.0, right_in[...])
    change = jnp.where(lane56 < 64, -0.5 * from_left, 0.5 * from_right)
    seam_slope[0:S, :] = change[0:S]
    seam_slope[S : S + 24, :] = change[0:24]
    seam_slope[72:80, :] = change[S:56]
    seam = slice(SEAM * 128, (SEAM + 1) * 128)

    def seam_value(d):
        ahead = pl.ds(d, S)
        return seam_field[0:S, :] * seam_slope[ahead, :] + seam_field[ahead, :] * seam_slope[0:S, :]

    def seam_pairs(d, carry):
        store(pl.ds(pl.multiple_of(d * S, S), S), seam, seam_value(d))
        return pairs_of((0, 7))(d, carry)

    other_pairs((0, 7))
    minus = seam_field[72:73, :] * seam_slope[0:S, :] + seam_field[0:S, :] * seam_slope[72:73, :]
    seam_back[...] = minus
    store(slice(0, S), seam, seam_field[0:S, :] * seam_slope[0:S, :])
    last_rows(seam, seam_value(24), minus)
    pair_high[:, 17 * 128 : LANES] = jnp.zeros((WIDE, 128), BF16)
    pair_low[:, 17 * 128 : LANES] = jnp.zeros((WIDE, 128), BF16)
    lax.fori_loop(1, 24, seam_pairs, 0)

    lax.fori_loop(0, 5, project_of(slice(INNER_LANES, LANES), True), 0)
    tensor[480:REGION, :] = jnp.zeros((REGION - 480, 128), F32)
    plane_start(tensor, part_b, 3)
    deep_start(moments, part_a, mine_a, deep_a, 0)
    gather_start(mine_a, deep_a, total_a, 0)
    deep_start(tensor, part_b, mine_b, deep_b, 3)

    gather_start(mine_b, deep_b, total_b, 3)
    gather_wait(part_a, 0)
    tail = total_a[432:480, :]
    second = jnp.where(lane < S, pltpu.roll(tail, 128 - 24, 1), 0.0) * (1.0 / R)
    gram_inv[...] = jnp.where(lane < S, pltpu.roll(tail, 128 - 72, 1), 0.0)
    mean_col = jnp.sum(jnp.where(lane == 120, tail, 0.0), axis=1, keepdims=True) * (1.0 / R)
    mean_row = jnp.sum(jnp.where(lane == sub, mean_col, 0.0), axis=0, keepdims=True)
    cov_inv[...] = second - mean_col * mean_row
    for lb in range(10):
        number = lb * 128 + lane
        first_d = lb * 128 // S
        d = jnp.full((S, 128), first_d, jnp.int32)
        for step in range(first_d + 1, first_d + 4):
            d = d + jnp.where(number >= step * S, 1, 0)
        k = number - d * S
        l = k + d
        l = jnp.where(l >= S, l - S, l)
        hot_k = jnp.where(sub == k, 1.0, 0.0)
        hot_l = jnp.where(sub == l, 1.0, 0.0)
        at_k = exact(second, tall(hot_k))
        at_l = exact(second, tall(hot_l))
        mean_k = jnp.sum(mean_col * hot_k, axis=0, keepdims=True)
        mean_l = jnp.sum(mean_col * hot_l, axis=0, keepdims=True)
        second_kl = jnp.sum(hot_k * at_l, axis=0, keepdims=True)
        third = total_a[lb * S : (lb + 1) * S, :] * (1.0 / R)
        third = third - mean_col * (second_kl - 2.0 * (mean_k * mean_l)) - mean_k * at_l - mean_l * at_k
        cov = second_kl - mean_k * mean_l
        if lb == 9:
            third = jnp.where(lane < 24, third, 0.0)
            cov = jnp.where(lane1 < 24, cov, 0.0)
        cube[lb * S : (lb + 1) * S, :] = third
        high, low = split(third)
        cube_split[0:S, lb * 128 : (lb + 1) * 128] = high
        cube_split[S : 2 * S, lb * 128 : (lb + 1) * 128] = low
        pair_cov[lb : lb + 1, :] = cov

    def contract(n, carry):
        cells = pl.ds(pl.multiple_of(n * 256, 256), 256)
        out = dot(cube_split[...], pair_high[:, cells])
        out = out[0:S] + out[S : 2 * S] + dot(cube_split[0:S, :], pair_low[:, cells])
        high, low = split(out)
        side_high[0:S, cells] = high
        side_low[0:S, cells] = low
        return carry

    def picked(at, values, axis):
        return jnp.sum(jnp.where(at, values, 0.0), axis=axis, keepdims=True)

    def eliminate(i, carry):
        p = 2 * i
        for matrix in (cov_inv, gram_inv):
            value = matrix[...]
            line_p, line_q = matrix[pl.ds(p, 1), :], matrix[pl.ds(p + 1, 1), :]
            at_p, at_q = lane1 == p, lane1 == p + 1
            a, b, d = picked(at_p, line_p, 1), picked(at_q, line_p, 1), picked(at_q, line_q, 1)
            column_p, column_q = picked(lane == p, value, 1), picked(lane == p + 1, value, 1)
            inverse = 1.0 / a
            ratio = b * inverse
            g = 1.0 / (d - b * ratio)
            f = -ratio * g
            e = inverse - ratio * f
            new_p = jnp.where(at_p, e, jnp.where(at_q, f, e * line_p + f * line_q))
            new_q = jnp.where(at_p, f, jnp.where(at_q, g, f * line_p + g * line_q))
            value = jnp.where((lane == p) | (lane == p + 1), 0.0, value)
            value = value - column_p * new_p - column_q * new_q
            matrix[...] = jnp.where(sub == p, new_p, jnp.where(sub == p + 1, new_q, value))
        return carry

    def contract_and_eliminate(n, carry):
        contract(n, carry)
        for k in range(3):
            eliminate(n * 3 + k, carry)
        return carry

    lax.fori_loop(0, 8, contract_and_eliminate, 0)
    contract(8, 0)

    for lb in range(10):
        value = exact(cov_inv[...], tall(cube[lb * S : (lb + 1) * S, :]))
        if lb == 9:
            value = jnp.where(lane == sub + 24, 1.0, value)
        high, low = split(value)
        key_high[0:S, lb * 128 : (lb + 1) * 128] = high
        key_low[0:S, lb * 128 : (lb + 1) * 128] = low
    key_high[S:128, :] = jnp.zeros((128 - S, WIDE), BF16)
    key_low[S:128, :] = jnp.zeros((128 - S, WIDE), BF16)

    def split3(value):
        high, low = split(value)
        lowest = (value - high.astype(F32) - low.astype(F32)).astype(BF16)
        return jnp.concatenate([high, low, lowest], axis=0)

    def product(factors, cells):
        out = dot(factors, side_high[:, cells])
        rest = dot(factors[0 : 2 * S], side_low[:, cells])
        return out[0:S] + out[S : 2 * S] + out[2 * S : 3 * S] + rest[0:S] + rest[S : 2 * S]

    from_cov = split3(cov_inv[...])
    from_gram = split3(pltpu.roll(gram_inv[...], 64, 1))
    seam_part = product(from_cov, slice(2048, LANES))[:, 0:128] + seam_back[...]
    for n in range(8):
        cells = slice(n * 256, (n + 1) * 256)
        out = product(from_cov, cells)
        high, low = split(product(from_gram, cells))
        side_high[64 : 64 + S, cells] = high
        side_low[64 : 64 + S, cells] = low
        for k in range(2):
            c, s = (INNER + OUTER)[2 * n + k]
            t = c * 8 + s
            part = back[t] + out[:, k * 128 : (k + 1) * 128]
            at_left = pltpu.roll(seam_part, 128 - t, 1) if t else seam_part
            part = part + jnp.where(lane == 0, at_left, 0.0)
            part = part + jnp.where(lane == 127, pltpu.roll(seam_part, 63 - t, 1), 0.0)
            half[t] = both[t, 0:S, :] - STEP * part
    centred = raw - mean_col
    pair_up(centred, False)
    gather_wait(part_b, 3)

    totals = split3(jnp.concatenate([total_b[lb * S : (lb + 1) * S, :] for lb in range(10)], axis=1))
    out = dot_nt(totals, key_high[...])
    rest = dot_nt(totals[0 : 2 * S], key_low[...])
    out = out[0:S] + out[S : 2 * S] + out[2 * S : 3 * S] + rest[0:S] + rest[S : 2 * S]
    from_sums = split3(pltpu.roll(tall(out).T[0:S], 64, 1))
    columns = jnp.zeros((S, 128), F32)
    for n in range(8):
        out = product(from_sums, slice(n * 256, (n + 1) * 256))
        for k in range(2):
            c, s = (INNER + OUTER)[2 * n + k]
            t = c * 8 + s
            value = half[t] - STEP * out[:, k * 128 : (k + 1) * 128]
            value = water[s : s + 1, :].astype(F32) * value
            half[t] = value
            columns = jnp.where(lane == 64 + t, pltpu.roll(value, 64 + t, 1), columns)
            columns = jnp.where(lane == t, pltpu.roll(value, t + 1, 1), columns)
            if s == 0:
                up_out2[c] = value
            if s == 7:
                down_out2[c] = value
    side_out2[...] = columns
    halo2 = copies(
        (up_out2, down_out2, side_out2, side_out2), (up_in2, down_in2, left_in2, right_in2), 4
    )
    for copy in halo2:
        copy.start()

    change = jnp.zeros((S, 128), F32)
    excess = jnp.zeros((S, 128), F32)
    for lb in range(10):
        here = total_b[lb * S : (lb + 1) * S, :]
        change = change + exact(here, pair_coeffs[lb * 128 : (lb + 1) * 128, :])
        excess = excess + here * pair_cov[lb : lb + 1, :]
    change = change - jnp.sum(excess, axis=1, keepdims=True)
    new_coeffs[...] = centred + STEP * exact(gram_inv[...], tall(change))

    for copy in halo2:
        copy.wait_recv()
    from_left = jnp.where(col == 0, 0.0, left_in2[...])
    from_right = jnp.where(col == COLS - 1, 0.0, right_in2[...])
    for t in range(16):
        c, s = divmod(t, 8)
        value = half[t]
        before = jnp.where(row == 0, 0.0, up_in2[c]) if s == 0 else half[t - 1]
        after = jnp.where(row == ROWS - 1, 0.0, down_in2[c]) if s == 7 else half[t + 1]
        ahead = jnp.where(lane == 127, pltpu.roll(from_right, 63 - t, 1), pltpu.roll(value, 127, 1))
        shifted = pltpu.roll(from_left, 128 - t, 1) if t else from_left
        behind = jnp.where(lane == 0, shifted, pltpu.roll(value, 1, 1))
        laplace = after + before + ahead + behind - 4.0 * value
        mask = water[s : s + 1, :].astype(F32)
        new_modes[pl.ds(t, S, stride=16), :] = mask * (value + VISCOUS * laplace)

    for copy in halo + halo2:
        copy.wait_send()
    sums_sent(part_a, deep_a, 0)
    sums_sent(part_b, deep_b, 3)


def on_device(modes, mean_flow, seeds, amplitudes, water_mask):
    vmem = pl.BlockSpec(memory_space=pltpu.VMEM)

    def f32(*shape):
        return pltpu.VMEM(shape, F32)

    def bf16(*shape):
        return pltpu.VMEM(shape, BF16)

    sums = [
        f32((GROUP - 1) * CHUNK, 128), f32((DEEP - 1) * CHUNK, 128), f32(2 * CHUNK, 128), f32(REGION, 128)
    ]
    new_modes, new_coeffs = pl.pallas_call(
        kernel,
        out_shape=(
            jax.ShapeDtypeStruct((S * 16, 128), F32),
            jax.ShapeDtypeStruct((S, 128), F32),
        ),
        in_specs=[pl.BlockSpec(memory_space=pltpu.MemorySpace.HBM)] * 5,
        out_specs=(vmem, vmem),
        scratch_shapes=[
            f32(S * 16, 128), f32(16, 128), pltpu.VMEM((S, 128), jnp.int32), f32(1, S), pltpu.VMEM((8, 128), jnp.int32),
            f32(16, 56, 128), f32(16, 72, 128), f32(16, 80, 128), f32(16, 80, 128), f32(16, S, 128),
            bf16(2 * S, LANES), bf16(WIDE, LANES), bf16(WIDE, LANES), bf16(128, LANES), bf16(128, LANES),
            f32(80, 128), f32(80, 128), f32(S, 128), f32(8, 128), f32(72, 128), f32(WIDE, 128),
            f32(REGION, 128), f32(REGION, 128), f32(480, 128), bf16(2 * S, WIDE),
            f32(16, 128), f32(S, 128), f32(S, 128), f32(16, S, 128), bf16(128, WIDE), bf16(128, WIDE),
            *sums, *sums,
            f32(2, 56, 128), f32(2, 56, 128), f32(56, 128), f32(2, 56, 128), f32(2, 56, 128), f32(56, 128), f32(56, 128),
            f32(2, S, 128), f32(2, S, 128), f32(S, 128), f32(2, S, 128), f32(2, S, 128), f32(S, 128), f32(S, 128),
            pltpu.SemaphoreType.DMA((8,)), pltpu.SemaphoreType.DMA((8,)),
            pltpu.SemaphoreType.DMA((6,)), pltpu.SemaphoreType.DMA((6,)), pltpu.SemaphoreType.DMA((5,)),
        ],
        compiler_params=pltpu.CompilerParams(
            collective_id=0, has_side_effects=True, vmem_limit_bytes=32 * 1024 * 1024
        ),
    )(
        *(
            pltpu.with_memory_space_constraint(value, pltpu.MemorySpace.HBM)
            for value in (
                modes.reshape(S * 16, 128),
                mean_flow.reshape(16, 128),
                seeds.T,
                amplitudes.reshape(1, S),
                water_mask,
            )
        )
    )
    return new_modes.reshape(S, 2, 8, 128), new_coeffs.T


def solution(mesh):
    return jax.shard_map(
        on_device,
        mesh=mesh,
        in_specs=(
            P(None, None, "row", "col"),
            P(None, "row", "col"),
            P(("row", "col"), None),
            P(),
            P("row", "col"),
        ),
        out_specs=(P(None, None, "row", "col"), P(("row", "col"), None)),
        check_vma=False,
    )
```

time: 57.3 us -> 46 us (0.80)
  Pallas kernels: 51.7 us -> 44 us
  local copies, waits for them, and re-layouts: 4.76 us -> 1.36 us
    pallas_call x1, Pallas kernels: 51.7 us -> 44 us  [on_device(): pl.pallas_call(kernel, out_shape=(jax.ShapeDtypeStruct((S * 16, 128), F32...]
    unnamed x3 -> x2, local copies, waits for them, and re-layouts: 4.76 us -> 1.36 us
where the time goes in v2:
time: 46 us
  Pallas kernels  44 us (96%)
  local copies, waits for them, and re-layouts  1.36 us (3%)
  between operations  0.64 us (1%)
    pallas_call x1, Pallas kernels, on_device(): pl.pallas_call(kernel, out_shape=(jax.ShapeDtypeStruct((S * 16, 128), F32...  44 us
    unnamed x2, local copies, waits for them, and re-layouts  1.36 us

profile of v2, /device:TPU:1, one launch (start us, length us, event | category | flops | bytes accessed | tf_op | source)
XLA Modules:
  0.0 46.0 jit_solution(14128485398469602558)
XLA Ops:
  0.6 44.0 %shard_map.68 = (f32[768,128]{1,0:T(8,128)S(1)}, f32[48,128]{1,0:T(8,128)S(1)}) custom-call(f32[768,128]{1,0:T(8,128)} %bitcast.8, f32[16,128]{1,0:T(8,128)} %bitcast.10, s32[48,128]{1,0:T(8,128)} %bitcast.9, f32[1,48]{1,0:T(1,128)} %bitcast.11, s32[8,128]{1,0:T(8,128)} %water_hbm.1), custom_call_target="tpu_custom_call" | custom-call | tf_op jit(solution)/shard_map/pallas_call | solution.py:583
  44.6 0.7 %copy.9 = f32[48,2,8,128]{3,2,1,0:T(8,128)} copy(f32[48,2,8,128]{3,2,1,0:T(8,128)S(1)} %bitcast.6) | data formatting | bytes 786432
  45.3 0.6 %copy.10 = f32[128,48]{0,1:T(8,128)} copy(f32[128,48]{0,1:T(8,128)S(1)} %bitcast.7) | data formatting | bytes 49152

commit v3 on v2

--- a/solution.py
+++ b/solution.py
@@ -22,6 +22,8 @@
 DEEP = COLS // ALONG_X
 CHUNK = 16
 REGION = GROUP * CHUNK
+HALF_CHUNK = CHUNK // 2
+HALF_REGION = GROUP * HALF_CHUNK
 PAIRS = 1176
 WIDE = 1280
 INNER = [(c, s) for s in range(1, 7) for c in range(2)]
@@ -29,7 +31,6 @@
 SLOT = {place: number for number, place in enumerate(INNER + OUTER)}
 SEAM = 16
 LANES = 18 * 128
-INNER_LANES = 12 * 128
 NT = (((1,), (1,)), ((), ()))
 
 
@@ -62,9 +63,9 @@
     modes_hbm, mean_hbm, seeds_hbm, amps_hbm, water_hbm, new_modes, new_coeffs,
     modes, mean, seeds, amps, water,
     base, both, grad_x, grad_y, back, weighted, pair_high, pair_low, side_high, side_low,
-    seam_field, seam_slope, seam_back, amp_row, coeffs, pair_coeffs, moments, tensor, cube, cube_split, pair_cov,
+    seam_field, seam_slope, seam_back, amp_row, coeffs, pair_coeffs, moments, tensor_b, tensor_c, cube, cube_split, pair_cov,
     cov_inv, gram_inv, half, key_high, key_low,
-    part_a, deep_a, mine_a, total_a, part_b, deep_b, mine_b, total_b,
+    part_a, deep_a, mine_a, total_a, part_b, deep_b, mine_b, total_b, part_c, deep_c, mine_c, total_c,
     up_out, down_out, side_out, up_in, down_in, left_in, right_in,
     up_out2, down_out2, side_out2, up_in2, down_in2, left_in2, right_in2,
     halo_send, halo_recv, sum_send, sum_recv, fetch_sem,
@@ -96,8 +97,10 @@
         pl.semaphore_signal(barrier, inc=1, device_id=deep(offset), device_id_type=MESH)
         return carry
 
-    lax.fori_loop(1, GROUP, greet_plane, 0)
-    lax.fori_loop(1, DEEP, greet_deep, 0)
+    for offset in range(1, GROUP):
+        greet_plane(offset, 0)
+    for offset in range(1, DEEP):
+        greet_deep(offset, 0)
     pl.semaphore_signal(barrier, inc=1, device_id=(row, left), device_id_type=MESH)
     pl.semaphore_signal(barrier, inc=1, device_id=(row, right), device_id_type=MESH)
 
@@ -130,12 +133,12 @@
             for k in range(4)
         ]
 
-    def plane_start(source, parts, sems):
+    def plane_start(source, parts, sems, chunk):
         def send(offset, carry):
             other, device = member(offset)
             pltpu.make_async_remote_copy(
-                src_ref=source.at[pl.ds(pl.multiple_of(other * CHUNK, CHUNK), CHUNK)],
-                dst_ref=parts.at[pl.ds(pl.multiple_of((offset - 1) * CHUNK, CHUNK), CHUNK)],
+                src_ref=source.at[pl.ds(pl.multiple_of(other * chunk, chunk), chunk)],
+                dst_ref=parts.at[pl.ds(pl.multiple_of((offset - 1) * chunk, chunk), chunk)],
                 send_sem=sum_send.at[sems],
                 recv_sem=sum_recv.at[sems],
                 device_id=device,
@@ -143,19 +146,20 @@
             ).start()
             return carry
 
-        lax.fori_loop(1, GROUP, send, 0)
-
-    def deep_start(source, parts, mine, deeper, sems):
+        for offset in range(1, GROUP):
+            send(offset, 0)
+
+    def deep_start(source, parts, mine, deeper, sems, chunk):
         pltpu.make_async_copy(parts, parts, sum_recv.at[sems]).wait()
-        value = source[pl.ds(pl.multiple_of(place * CHUNK, CHUNK), CHUNK), :]
+        value = source[pl.ds(pl.multiple_of(place * chunk, chunk), chunk), :]
         for k in range(GROUP - 1):
-            value = value + parts[k * CHUNK : (k + 1) * CHUNK, :]
-        mine[0:CHUNK, :] = value
+            value = value + parts[k * chunk : (k + 1) * chunk, :]
+        mine[0:chunk, :] = value
 
         def send(offset, carry):
             pltpu.make_async_remote_copy(
-                src_ref=mine.at[pl.ds(0, CHUNK)],
-                dst_ref=deeper.at[pl.ds(pl.multiple_of((offset - 1) * CHUNK, CHUNK), CHUNK)],
+                src_ref=mine.at[pl.ds(0, chunk)],
+                dst_ref=deeper.at[pl.ds(pl.multiple_of((offset - 1) * chunk, chunk), chunk)],
                 send_sem=sum_send.at[sems + 1],
                 recv_sem=sum_recv.at[sems + 1],
                 device_id=deep(offset),
@@ -163,20 +167,21 @@
             ).start()
             return carry
 
-        lax.fori_loop(1, DEEP, send, 0)
-
-    def gather_start(mine, deeper, total, sems):
+        for offset in range(1, DEEP):
+            send(offset, 0)
+
+    def gather_start(mine, deeper, total, sems, chunk):
         pltpu.make_async_copy(deeper, deeper, sum_recv.at[sems + 1]).wait()
-        value = mine[0:CHUNK, :]
+        value = mine[0:chunk, :]
         for k in range(DEEP - 1):
-            value = value + deeper[k * CHUNK : (k + 1) * CHUNK, :]
-        mine[CHUNK : 2 * CHUNK, :] = value
-        own = pl.ds(pl.multiple_of(place * CHUNK, CHUNK), CHUNK)
+            value = value + deeper[k * chunk : (k + 1) * chunk, :]
+        mine[chunk : 2 * chunk, :] = value
+        own = pl.ds(pl.multiple_of(place * chunk, chunk), chunk)
         total[own, :] = value
 
         def send(offset, carry):
             pltpu.make_async_remote_copy(
-                src_ref=mine.at[pl.ds(CHUNK, CHUNK)],
+                src_ref=mine.at[pl.ds(chunk, chunk)],
                 dst_ref=total.at[own],
                 send_sem=sum_send.at[sems + 2],
                 recv_sem=sum_recv.at[sems + 2],
@@ -185,7 +190,8 @@
             ).start()
             return carry
 
-        lax.fori_loop(1, GROUP, send, 0)
+        for offset in range(1, GROUP):
+            send(offset, 0)
 
     def gather_wait(parts, sems):
         pltpu.make_async_copy(parts, parts, sum_recv.at[sems + 2]).wait()
@@ -293,7 +299,7 @@
     )
     for copy in halo:
         copy.start()
-    plane_start(moments, part_a, 0)
+    plane_start(moments, part_a, 0, CHUNK)
 
     def pair_value(d, t, u0, u1, v0, v1):
         ahead = pl.ds(d, S)
@@ -307,14 +313,23 @@
         pair_high[rows, lanes] = high
         pair_low[rows, lanes] = low
 
-    def pairs_of(grid_rows):
-        def pair_block(d, carry):
-            rows = pl.ds(pl.multiple_of(d * S, S), S)
+    def pairs_of(grid_rows, together):
+        def pair_block(first, carry):
             for s in grid_rows:
                 u0, u1 = both[s, 0:S, :], both[8 + s, 0:S, :]
-                v0, v1 = both[s, pl.ds(d, S), :], both[8 + s, pl.ds(d, S), :]
-                for c in range(2):
-                    store(rows, lanes_of(c, s), pair_value(d, c * 8 + s, u0, u1, v0, v1))
+                slopes = [(grad_x[c * 8 + s, 0:S, :], grad_y[c * 8 + s, 0:S, :]) for c in range(2)]
+                for k in range(together):
+                    d = first + k
+                    rows = pl.ds(pl.multiple_of(d * S, S), S)
+                    ahead = pl.ds(d, S)
+                    v0, v1 = both[s, ahead, :], both[8 + s, ahead, :]
+                    for c in range(2):
+                        t = c * 8 + s
+                        value = (
+                            u0 * grad_x[t, ahead, :] + u1 * grad_y[t, ahead, :]
+                            + v0 * slopes[c][0] + v1 * slopes[c][1]
+                        )
+                        store(rows, lanes_of(c, s), value)
             return carry
 
         return pair_block
@@ -338,22 +353,17 @@
                 back[t] = minus
                 last_rows(lanes_of(c, s), pair_value(24, t, u0, u1, v0, v1), minus)
 
-    def project_of(lanes, add):
-        def project(lb, carry):
-            rows = pl.ds(pl.multiple_of(lb * 256, 256), 256)
-            out = dot_nt(weighted[:, lanes], pair_high[rows, lanes])
-            out = out[0:S] + out[S : 2 * S] + dot_nt(weighted[0:S, lanes], pair_low[rows, lanes])
-            for k in range(2):
-                to = pl.ds(pl.multiple_of(lb * 96 + k * S, S), S)
-                part = out[:, k * 128 : (k + 1) * 128]
-                tensor[to, :] = tensor[to, :] + part if add else part
-            return carry
-
-        return project
+    def project(first, count, target):
+        rows = slice(first, first + count)
+        out = dot_nt(weighted[...], pair_high[rows, :])
+        out = out[0:S] + out[S : 2 * S] + dot_nt(weighted[0:S, :], pair_low[rows, :])
+        for k in range(count // 128):
+            to = (first // 128 + k) % 5 * S
+            target[to : to + S, :] = out[:, k * 128 : (k + 1) * 128]
 
     other_pairs(range(1, 7))
-    lax.fori_loop(1, 24, pairs_of(range(1, 7)), 0)
-    lax.fori_loop(0, 5, project_of(slice(0, INNER_LANES), False), 0)
+    pairs_of(range(1, 7), 1)(1, 0)
+    lax.fori_loop(1, 12, lambda i, carry: pairs_of(range(1, 7), 2)(2 * i, carry), 0)
 
     for copy in halo:
         copy.wait_recv()
@@ -372,9 +382,10 @@
         ahead = pl.ds(d, S)
         return seam_field[0:S, :] * seam_slope[ahead, :] + seam_field[ahead, :] * seam_slope[0:S, :]
 
-    def seam_pairs(d, carry):
-        store(pl.ds(pl.multiple_of(d * S, S), S), seam, seam_value(d))
-        return pairs_of((0, 7))(d, carry)
+    def outer_pairs(i, carry):
+        for k in range(2):
+            store(pl.ds(pl.multiple_of((2 * i + k) * S, S), S), seam, seam_value(2 * i + k))
+        return pairs_of((0, 7), 2)(2 * i, carry)
 
     other_pairs((0, 7))
     minus = seam_field[72:73, :] * seam_slope[0:S, :] + seam_field[0:S, :] * seam_slope[72:73, :]
@@ -383,16 +394,28 @@
     last_rows(seam, seam_value(24), minus)
     pair_high[:, 17 * 128 : LANES] = jnp.zeros((WIDE, 128), BF16)
     pair_low[:, 17 * 128 : LANES] = jnp.zeros((WIDE, 128), BF16)
-    lax.fori_loop(1, 24, seam_pairs, 0)
-
-    lax.fori_loop(0, 5, project_of(slice(INNER_LANES, LANES), True), 0)
-    tensor[480:REGION, :] = jnp.zeros((REGION - 480, 128), F32)
-    plane_start(tensor, part_b, 3)
-    deep_start(moments, part_a, mine_a, deep_a, 0)
-    gather_start(mine_a, deep_a, total_a, 0)
-    deep_start(tensor, part_b, mine_b, deep_b, 3)
-
-    gather_start(mine_b, deep_b, total_b, 3)
+    store(slice(S, 2 * S), seam, seam_value(1))
+    pairs_of((0, 7), 1)(1, 0)
+    lax.fori_loop(1, 7, outer_pairs, 0)
+    project(0, 256, tensor_b)
+    project(256, 256, tensor_b)
+    project(512, 128, tensor_b)
+    tensor_b[240:HALF_REGION, :] = jnp.zeros((HALF_REGION - 240, 128), F32)
+    plane_start(tensor_b, part_b, 3, HALF_CHUNK)
+    deep_start(moments, part_a, mine_a, deep_a, 0, CHUNK)
+
+    lax.fori_loop(7, 12, outer_pairs, 0)
+    project(640, 128, tensor_c)
+    project(768, 256, tensor_c)
+    project(1024, 256, tensor_c)
+    tensor_c[240:HALF_REGION, :] = jnp.zeros((HALF_REGION - 240, 128), F32)
+    plane_start(tensor_c, part_c, 6, HALF_CHUNK)
+    deep_start(tensor_b, part_b, mine_b, deep_b, 3, HALF_CHUNK)
+    gather_start(mine_a, deep_a, total_a, 0, CHUNK)
+    deep_start(tensor_c, part_c, mine_c, deep_c, 6, HALF_CHUNK)
+
+    gather_start(mine_b, deep_b, total_b, 3, HALF_CHUNK)
+    gather_start(mine_c, deep_c, total_c, 6, HALF_CHUNK)
     gather_wait(part_a, 0)
     tail = total_a[432:480, :]
     second = jnp.where(lane < S, pltpu.roll(tail, 128 - 24, 1), 0.0) * (1.0 / R)
@@ -469,8 +492,18 @@
     lax.fori_loop(0, 8, contract_and_eliminate, 0)
     contract(8, 0)
 
+    def split3(value):
+        high, low = split(value)
+        lowest = (value - high.astype(F32) - low.astype(F32)).astype(BF16)
+        return jnp.concatenate([high, low, lowest], axis=0)
+
+    from_cov = split3(cov_inv[...])
+    from_gram = split3(pltpu.roll(gram_inv[...], 64, 1))
+    out = dot(from_cov[:, 0:S], cube_split[0:S, :])
+    rest = dot(from_cov[0 : 2 * S, 0:S], cube_split[S : 2 * S, :])
+    keys = out[0:S] + out[S : 2 * S] + out[2 * S : 3 * S] + rest[0:S] + rest[S : 2 * S]
     for lb in range(10):
-        value = exact(cov_inv[...], tall(cube[lb * S : (lb + 1) * S, :]))
+        value = keys[:, lb * 128 : (lb + 1) * 128]
         if lb == 9:
             value = jnp.where(lane == sub + 24, 1.0, value)
         high, low = split(value)
@@ -479,18 +512,11 @@
     key_high[S:128, :] = jnp.zeros((128 - S, WIDE), BF16)
     key_low[S:128, :] = jnp.zeros((128 - S, WIDE), BF16)
 
-    def split3(value):
-        high, low = split(value)
-        lowest = (value - high.astype(F32) - low.astype(F32)).astype(BF16)
-        return jnp.concatenate([high, low, lowest], axis=0)
-
     def product(factors, cells):
         out = dot(factors, side_high[:, cells])
         rest = dot(factors[0 : 2 * S], side_low[:, cells])
         return out[0:S] + out[S : 2 * S] + out[2 * S : 3 * S] + rest[0:S] + rest[S : 2 * S]
 
-    from_cov = split3(cov_inv[...])
-    from_gram = split3(pltpu.roll(gram_inv[...], 64, 1))
     seam_part = product(from_cov, slice(2048, LANES))[:, 0:128] + seam_back[...]
     for n in range(8):
         cells = slice(n * 256, (n + 1) * 256)
@@ -506,17 +532,22 @@
             part = part + jnp.where(lane == 0, at_left, 0.0)
             part = part + jnp.where(lane == 127, pltpu.roll(seam_part, 63 - t, 1), 0.0)
             half[t] = both[t, 0:S, :] - STEP * part
-    centred = raw - mean_col
-    pair_up(centred, False)
     gather_wait(part_b, 3)
-
-    totals = split3(jnp.concatenate([total_b[lb * S : (lb + 1) * S, :] for lb in range(10)], axis=1))
+    gather_wait(part_c, 6)
+
+    def summed(lb):
+        return (total_b if lb < 5 else total_c)[lb % 5 * S : (lb % 5 + 1) * S, :]
+
+    totals = split3(jnp.concatenate([summed(lb) for lb in range(10)], axis=1))
     out = dot_nt(totals, key_high[...])
     rest = dot_nt(totals[0 : 2 * S], key_low[...])
     out = out[0:S] + out[S : 2 * S] + out[2 * S : 3 * S] + rest[0:S] + rest[S : 2 * S]
     from_sums = split3(pltpu.roll(tall(out).T[0:S], 64, 1))
+    halo2 = copies(
+        (up_out2, down_out2, side_out2, side_out2), (up_in2, down_in2, left_in2, right_in2), 4
+    )
     columns = jnp.zeros((S, 128), F32)
-    for n in range(8):
+    for n in (6, 7, 0, 1, 2, 3, 4, 5):
         out = product(from_sums, slice(n * 256, (n + 1) * 256))
         for k in range(2):
             c, s = (INNER + OUTER)[2 * n + k]
@@ -530,17 +561,19 @@
                 up_out2[c] = value
             if s == 7:
                 down_out2[c] = value
+        if n == 7:
+            for copy in halo2[0:2]:
+                copy.start()
     side_out2[...] = columns
-    halo2 = copies(
-        (up_out2, down_out2, side_out2, side_out2), (up_in2, down_in2, left_in2, right_in2), 4
-    )
-    for copy in halo2:
+    for copy in halo2[2:4]:
         copy.start()
 
+    centred = raw - mean_col
+    pair_up(centred, False)
     change = jnp.zeros((S, 128), F32)
     excess = jnp.zeros((S, 128), F32)
     for lb in range(10):
-        here = total_b[lb * S : (lb + 1) * S, :]
+        here = summed(lb)
         change = change + exact(here, pair_coeffs[lb * 128 : (lb + 1) * 128, :])
         excess = excess + here * pair_cov[lb : lb + 1, :]
     change = change - jnp.sum(excess, axis=1, keepdims=True)
@@ -566,6 +599,7 @@
         copy.wait_send()
     sums_sent(part_a, deep_a, 0)
     sums_sent(part_b, deep_b, 3)
+    sums_sent(part_c, deep_c, 6)
 
 
 def on_device(modes, mean_flow, seeds, amplitudes, water_mask):
@@ -577,9 +611,11 @@
     def bf16(*shape):
         return pltpu.VMEM(shape, BF16)
 
-    sums = [
-        f32((GROUP - 1) * CHUNK, 128), f32((DEEP - 1) * CHUNK, 128), f32(2 * CHUNK, 128), f32(REGION, 128)
-    ]
+    def sums(chunk):
+        return [
+            f32((GROUP - 1) * chunk, 128), f32((DEEP - 1) * chunk, 128), f32(2 * chunk, 128), f32(GROUP * chunk, 128)
+        ]
+
     new_modes, new_coeffs = pl.pallas_call(
         kernel,
         out_shape=(
@@ -593,13 +629,13 @@
             f32(16, 56, 128), f32(16, 72, 128), f32(16, 80, 128), f32(16, 80, 128), f32(16, S, 128),
             bf16(2 * S, LANES), bf16(WIDE, LANES), bf16(WIDE, LANES), bf16(128, LANES), bf16(128, LANES),
             f32(80, 128), f32(80, 128), f32(S, 128), f32(8, 128), f32(72, 128), f32(WIDE, 128),
-            f32(REGION, 128), f32(REGION, 128), f32(480, 128), bf16(2 * S, WIDE),
+            f32(REGION, 128), f32(HALF_REGION, 128), f32(HALF_REGION, 128), f32(480, 128), bf16(2 * S, WIDE),
             f32(16, 128), f32(S, 128), f32(S, 128), f32(16, S, 128), bf16(128, WIDE), bf16(128, WIDE),
-            *sums, *sums,
+            *sums(CHUNK), *sums(HALF_CHUNK), *sums(HALF_CHUNK),
             f32(2, 56, 128), f32(2, 56, 128), f32(56, 128), f32(2, 56, 128), f32(2, 56, 128), f32(56, 128), f32(56, 128),
             f32(2, S, 128), f32(2, S, 128), f32(S, 128), f32(2, S, 128), f32(2, S, 128), f32(S, 128), f32(S, 128),
             pltpu.SemaphoreType.DMA((8,)), pltpu.SemaphoreType.DMA((8,)),
-            pltpu.SemaphoreType.DMA((6,)), pltpu.SemaphoreType.DMA((6,)), pltpu.SemaphoreType.DMA((5,)),
+            pltpu.SemaphoreType.DMA((9,)), pltpu.SemaphoreType.DMA((9,)), pltpu.SemaphoreType.DMA((5,)),
         ],
         compiler_params=pltpu.CompilerParams(
             collective_id=0, has_side_effects=True, vmem_limit_bytes=32 * 1024 * 1024

time: 46 us -> 44.4 us (0.965)
  Pallas kernels: 44 us -> 42.3 us
    pallas_call x1, Pallas kernels: 44 us -> 42.3 us  [on_device(): pl.pallas_call(kernel, out_shape=(jax.ShapeDtypeStruct((S * 16, 128), F32...]
where the time goes in v3:
time: 44.4 us; the launch traced here: 44.3 us
  Pallas kernels  42.3 us (95%)
  local copies, waits for them, and re-layouts  1.36 us (3%)
  between operations  0.64 us (1%)
    pallas_call x1, Pallas kernels, on_device(): pl.pallas_call(kernel, out_shape=(jax.ShapeDtypeStruct((S * 16, 128), F32...  42.3 us
    unnamed x2, local copies, waits for them, and re-layouts  1.36 us

profile of v3, /device:TPU:1, one launch (start us, length us, event | category | flops | bytes accessed | tf_op | source)
XLA Modules:
  0.0 44.3 jit_solution(6751901366316163769)
XLA Ops:
  0.6 42.3 %shard_map.68 = (f32[768,128]{1,0:T(8,128)S(1)}, f32[48,128]{1,0:T(8,128)S(1)}) custom-call(f32[768,128]{1,0:T(8,128)} %bitcast.8, f32[16,128]{1,0:T(8,128)} %bitcast.10, s32[48,128]{1,0:T(8,128)} %bitcast.9, f32[1,48]{1,0:T(1,128)} %bitcast.11, s32[8,128]{1,0:T(8,128)} %water_hbm.1), custom_call_target="tpu_custom_call" | custom-call | tf_op jit(solution)/shard_map/pallas_call | solution.py:619
  43.0 0.7 %copy.9 = f32[48,2,8,128]{3,2,1,0:T(8,128)} copy(f32[48,2,8,128]{3,2,1,0:T(8,128)S(1)} %bitcast.6) | data formatting | bytes 786432
  43.7 0.6 %copy.10 = f32[128,48]{0,1:T(8,128)} copy(f32[128,48]{0,1:T(8,128)S(1)} %bitcast.7) | data formatting | bytes 49152

commit v4 on v3

--- a/solution.py
+++ b/solution.py
@@ -313,6 +313,9 @@
         pair_high[rows, lanes] = high
         pair_low[rows, lanes] = low
 
+    def block_rows(d):
+        return slice(d * S, (d + 1) * S) if isinstance(d, int) else pl.ds(pl.multiple_of(d * S, S), S)
+
     def pairs_of(grid_rows, together):
         def pair_block(first, carry):
             for s in grid_rows:
@@ -320,7 +323,7 @@
                 slopes = [(grad_x[c * 8 + s, 0:S, :], grad_y[c * 8 + s, 0:S, :]) for c in range(2)]
                 for k in range(together):
                     d = first + k
-                    rows = pl.ds(pl.multiple_of(d * S, S), S)
+                    rows = block_rows(d)
                     ahead = pl.ds(d, S)
                     v0, v1 = both[s, ahead, :], both[8 + s, ahead, :]
                     for c in range(2):
@@ -384,7 +387,7 @@
 
     def outer_pairs(i, carry):
         for k in range(2):
-            store(pl.ds(pl.multiple_of((2 * i + k) * S, S), S), seam, seam_value(2 * i + k))
+            store(block_rows(2 * i + k), seam, seam_value(2 * i + k))
         return pairs_of((0, 7), 2)(2 * i, carry)
 
     other_pairs((0, 7))
@@ -400,11 +403,12 @@
     project(0, 256, tensor_b)
     project(256, 256, tensor_b)
     project(512, 128, tensor_b)
+    for i in range(7, 12):
+        outer_pairs(i, 0)
     tensor_b[240:HALF_REGION, :] = jnp.zeros((HALF_REGION - 240, 128), F32)
     plane_start(tensor_b, part_b, 3, HALF_CHUNK)
     deep_start(moments, part_a, mine_a, deep_a, 0, CHUNK)
 
-    lax.fori_loop(7, 12, outer_pairs, 0)
     project(640, 128, tensor_c)
     project(768, 256, tensor_c)
     project(1024, 256, tensor_c)
@@ -423,6 +427,12 @@
     mean_col = jnp.sum(jnp.where(lane == 120, tail, 0.0), axis=1, keepdims=True) * (1.0 / R)
     mean_row = jnp.sum(jnp.where(lane == sub, mean_col, 0.0), axis=0, keepdims=True)
     cov_inv[...] = second - mean_col * mean_row
+    def split3(value):
+        high, low = split(value)
+        lowest = (value - high.astype(F32) - low.astype(F32)).astype(BF16)
+        return jnp.concatenate([high, low, lowest], axis=0)
+
+    spread = split3(second)
     for lb in range(10):
         number = lb * 128 + lane
         first_d = lb * 128 // S
@@ -434,8 +444,10 @@
         l = jnp.where(l >= S, l - S, l)
         hot_k = jnp.where(sub == k, 1.0, 0.0)
         hot_l = jnp.where(sub == l, 1.0, 0.0)
-        at_k = exact(second, tall(hot_k))
-        at_l = exact(second, tall(hot_l))
+        hot = jnp.concatenate([tall(hot_k), tall(hot_l)], axis=1).astype(BF16)
+        out = dot(spread, hot)
+        out = out[0:S] + out[S : 2 * S] + out[2 * S : 3 * S]
+        at_k, at_l = out[:, 0:128], out[:, 128:256]
         mean_k = jnp.sum(mean_col * hot_k, axis=0, keepdims=True)
         mean_l = jnp.sum(mean_col * hot_l, axis=0, keepdims=True)
         second_kl = jnp.sum(hot_k * at_l, axis=0, keepdims=True)
@@ -491,11 +503,6 @@
 
     lax.fori_loop(0, 8, contract_and_eliminate, 0)
     contract(8, 0)
-
-    def split3(value):
-        high, low = split(value)
-        lowest = (value - high.astype(F32) - low.astype(F32)).astype(BF16)
-        return jnp.concatenate([high, low, lowest], axis=0)
 
     from_cov = split3(cov_inv[...])
     from_gram = split3(pltpu.roll(gram_inv[...], 64, 1))

time: 44.4 us -> 44.3 us (level)
  no operation moved by 1% of the time
where the time goes in v4:
time: 44.3 us; the launch traced here: 44.2 us
  Pallas kernels  42.2 us (95%)
  local copies, waits for them, and re-layouts  1.36 us (3%)
  between operations  0.64 us (1%)
    pallas_call x1, Pallas kernels, on_device(): pl.pallas_call(kernel, out_shape=(jax.ShapeDtypeStruct((S * 16, 128), F32...  42.2 us
    unnamed x2, local copies, waits for them, and re-layouts  1.36 us

profile of v4, /device:TPU:1, one launch (start us, length us, event | category | flops | bytes accessed | tf_op | source)
XLA Modules:
  0.0 44.2 jit_solution(5270789297775376804)
XLA Ops:
  0.6 42.2 %shard_map.68 = (f32[768,128]{1,0:T(8,128)S(1)}, f32[48,128]{1,0:T(8,128)S(1)}) custom-call(f32[768,128]{1,0:T(8,128)} %bitcast.8, f32[16,128]{1,0:T(8,128)} %bitcast.10, s32[48,128]{1,0:T(8,128)} %bitcast.9, f32[1,48]{1,0:T(1,128)} %bitcast.11, s32[8,128]{1,0:T(8,128)} %water_hbm.1), custom_call_target="tpu_custom_call" | custom-call | tf_op jit(solution)/shard_map/pallas_call | solution.py:626
  42.8 0.7 %copy.9 = f32[48,2,8,128]{3,2,1,0:T(8,128)} copy(f32[48,2,8,128]{3,2,1,0:T(8,128)S(1)} %bitcast.6) | data formatting | bytes 786432
  43.6 0.6 %copy.10 = f32[128,48]{0,1:T(8,128)} copy(f32[128,48]{0,1:T(8,128)S(1)} %bitcast.7) | data formatting | bytes 49152

commit v5 on v4

--- a/solution.py
+++ b/solution.py
@@ -368,11 +368,15 @@
     pairs_of(range(1, 7), 1)(1, 0)
     lax.fori_loop(1, 12, lambda i, carry: pairs_of(range(1, 7), 2)(2 * i, carry), 0)
 
-    for copy in halo:
+    for copy in halo[0:2]:
         copy.wait_recv()
     for c in range(2):
         slope(c * 8, jnp.where(row == 0, 0.0, up_in[c]), base[c * 8 + 1])
         slope(c * 8 + 7, base[c * 8 + 6], jnp.where(row == ROWS - 1, 0.0, down_in[c]))
+    other_pairs((0, 7))
+    pairs_of((0, 7), 1)(1, 0)
+    for copy in halo[2:4]:
+        copy.wait_recv()
     from_left = jnp.where(col == 0, 0.0, left_in[...])
     from_right = jnp.where(col == COLS - 1, 0.0, right_in[...])
     change = jnp.where(lane56 < 64, -0.5 * from_left, 0.5 * from_right)
@@ -390,7 +394,6 @@
             store(block_rows(2 * i + k), seam, seam_value(2 * i + k))
         return pairs_of((0, 7), 2)(2 * i, carry)
 
-    other_pairs((0, 7))
     minus = seam_field[72:73, :] * seam_slope[0:S, :] + seam_field[0:S, :] * seam_slope[72:73, :]
     seam_back[...] = minus
     store(slice(0, S), seam, seam_field[0:S, :] * seam_slope[0:S, :])
@@ -398,7 +401,6 @@
     pair_high[:, 17 * 128 : LANES] = jnp.zeros((WIDE, 128), BF16)
     pair_low[:, 17 * 128 : LANES] = jnp.zeros((WIDE, 128), BF16)
     store(slice(S, 2 * S), seam, seam_value(1))
-    pairs_of((0, 7), 1)(1, 0)
     lax.fori_loop(1, 7, outer_pairs, 0)
     project(0, 256, tensor_b)
     project(256, 256, tensor_b)

time: 44.3 us -> 44.1 us (level)
  no operation moved by 1% of the time
where the time goes in v5:
time: 44.1 us; the launch traced here: 44 us
  Pallas kernels  42.1 us (95%)
  local copies, waits for them, and re-layouts  1.36 us (3%)
  between operations  0.64 us (1%)
    pallas_call x1, Pallas kernels, on_device(): pl.pallas_call(kernel, out_shape=(jax.ShapeDtypeStruct((S * 16, 128), F32...  42.1 us
    unnamed x2, local copies, waits for them, and re-layouts  1.36 us

profile of v5, /device:TPU:1, one launch (start us, length us, event | category | flops | bytes accessed | tf_op | source)
XLA Modules:
  0.0 44.0 jit_solution(11817867670822465641)
XLA Ops:
  0.6 42.1 %shard_map.68 = (f32[768,128]{1,0:T(8,128)S(1)}, f32[48,128]{1,0:T(8,128)S(1)}) custom-call(f32[768,128]{1,0:T(8,128)} %bitcast.8, f32[16,128]{1,0:T(8,128)} %bitcast.10, s32[48,128]{1,0:T(8,128)} %bitcast.9, f32[1,48]{1,0:T(1,128)} %bitcast.11, s32[8,128]{1,0:T(8,128)} %water_hbm.1), custom_call_target="tpu_custom_call" | custom-call | tf_op jit(solution)/shard_map/pallas_call | solution.py:628
  42.7 0.7 %copy.9 = f32[48,2,8,128]{3,2,1,0:T(8,128)} copy(f32[48,2,8,128]{3,2,1,0:T(8,128)S(1)} %bitcast.6) | data formatting | bytes 786432
  43.4 0.6 %copy.10 = f32[128,48]{0,1:T(8,128)} copy(f32[128,48]{0,1:T(8,128)S(1)} %bitcast.7) | data formatting | bytes 49152
